TPU v7x, 1024 devices: a whole 8x8x8 slice. The times are simulated.
1024 devices in a mesh: row: 8 (over z_lo, core), col: 128 (over y, x, z_hi).
Axes of the slice: x: 8, y: 8, z: 8 (z_hi: 2, z_lo: 4; z = z_hi * 4 + z_lo), core: 2. Of those that a mesh axis runs over, the one named last changes fastest.
Arguments:
- basis_block: float32 [32, 131072], P(None, ('row', 'col')), may hold values from -40 to 40
- previous: float32 [32, 131072], P(None, ('row', 'col')), may hold values from -6 to 6
- coupling: float32 [32, 32], replicated, may hold values from -2 to 2, as said below
- energies: float32 [131072], P(('row', 'col')), may hold values from 0.5 to 5
- tile_values: float32 [8, 128, 16, 128, 128], P('row', 'col'), may hold values from -0.125 to 0.125
- tile_rows: int32 [8, 128, 16], P('row', 'col'), may hold values from 0 to 127, as said below
- tile_cols: int32 [8, 128, 16], P('row', 'col'), may hold values from 0 to 7
- counts: int32 [8, 128], P('row', 'col'), may hold values from 12 to 16, as said below
Outputs:
- alpha_block: float32 [32, 32], replicated
- beta_block: float32 [32, 32], replicated
- basis_next: float32 [32, 131072], P(None, ('row', 'col'))
Inputs may be any that keep to these rules, and one draw needn't show every extreme that they name: `coupling`: upper triangular with a positive diagonal. Slots 0 to counts - 1 of a device hold its tiles, the others are unused; some device has all 16 slots live. `tile_rows`: the first min(16, 128) slots of a device name different tile rows; beyond those, slots of one device may name the same tile position and their tiles then add.
All inputs are finite; a program needn't handle non-finite values.
Results may differ from a plain program's by a relative error of at most 0.0003.
Values sent between devices are 32-bit elements; how exact they have to be, the bound alone decides.
A program may use at most 32 MiB of HBM per device.

v0:
```python
import jax
import jax.numpy as jnp
from jax import lax
from jax.sharding import Mesh
from jax.sharding import PartitionSpec as P

ROW = ("row_0", "row_1")
COL = ("col_0", "col_1", "col_2")
ROW_COL = ("row_0", "row_1", "col_0", "col_1", "col_2")


def from_everyone(value, axis):
    copies = jnp.broadcast_to(value, (lax.axis_size(axis), *value.shape))
    return lax.all_to_all(copies, axis, split_axis=0, concat_axis=0, tiled=True)


def joined_along(parts, dim):
    dims = list(parts.shape[1:])
    dims[dim] *= parts.shape[0]
    return jnp.moveaxis(parts, 0, dim).reshape(dims)


def gathered_copies(value, axis, dim):
    parts = from_everyone(value, axis)
    return joined_along(parts, dim)


def sum_by_axis(subtotal, axes):
    for axis in axes:
        subtotal = lax.psum_scatter(subtotal, axis, scatter_dimension=0, tiled=True)
    return subtotal


def in_blocks(value, dim, count):
    dims = value.shape
    parts = value.reshape(*dims[:dim], count, dims[dim] // count, *dims[dim + 1 :])
    return jnp.moveaxis(parts, dim, 0)


def sent_and_summed(value, axis, dim):
    parts = in_blocks(value, dim, lax.axis_size(axis))
    arrived = lax.all_to_all(parts, axis, split_axis=0, concat_axis=0, tiled=True)
    return arrived.sum(axis=0)


def by_axis(value, axes):
    for axis in axes:
        value = lax.psum(value, axis)
    return value


def inner_block(left_rows, right_rows):
    return jnp.dot(
        left_rows, right_rows.T, precision=lax.Precision.HIGHEST, preferred_element_type=jnp.float32
    )


def shards(basis_block, previous, coupling, energies, tile_values, tile_rows, tile_cols, counts):
    highest = lax.Precision.HIGHEST
    vec_count = basis_block.shape[0]
    piece_len = basis_block.shape[1]
    slot_count = tile_values.shape[2]
    tile_len = tile_values.shape[-1]
    piece_tiles = piece_len // tile_len
    state_count = piece_len * lax.axis_size(ROW) * lax.axis_size(COL)
    stacked = basis_block.reshape(vec_count, piece_tiles, tile_len).transpose(1, 0, 2)
    row_states = lax.all_gather(stacked, COL, axis=0, tiled=True)
    col_states = gathered_copies(stacked, ROW, 0)
    tile_set = tile_values.reshape(slot_count, tile_len, tile_len)
    slot_rows = tile_rows.reshape(slot_count)
    slot_cols = tile_cols.reshape(slot_count)
    live_mask = (jnp.arange(slot_count) < counts.reshape(())).astype(jnp.float32)[:, None, None]
    picked_cols = jnp.take(col_states, slot_cols, axis=0)
    picked_rows = jnp.take(row_states, slot_rows, axis=0)
    direct = (
        jnp.einsum(
            "sij,skj->ski",
            tile_set,
            picked_cols,
            precision=highest,
            preferred_element_type=jnp.float32,
        )
        * live_mask
    )
    mirror = (
        jnp.einsum(
            "sij,ski->skj",
            tile_set,
            picked_rows,
            precision=highest,
            preferred_element_type=jnp.float32,
        )
        * live_mask
    )
    row_count = piece_tiles * lax.axis_size(COL)
    inside = (slot_rows >= 0) & (slot_rows < row_count)
    segment_ids = jnp.where(inside, slot_rows, row_count)
    own_direct = sum_by_axis(
        jax.ops.segment_sum(direct, segment_ids, num_segments=row_count + 1)[:row_count], COL
    )
    col_sums = jax.ops.segment_sum(mirror, slot_cols, num_segments=col_states.shape[0])
    own_mirror = sent_and_summed(col_sums, ROW, 0)
    offdiag_part = (own_direct + own_mirror).transpose(1, 0, 2).reshape(vec_count, piece_len)
    applied = (
        energies[None, :] * basis_block
        + offdiag_part
        - jnp.dot(coupling, previous, precision=highest, preferred_element_type=jnp.float32)
    )
    cross_sum, image_sum, basis_sum = (
        by_axis(inner_block(basis_block, applied), ROW_COL),
        by_axis(inner_block(applied, applied), ROW_COL),
        by_axis(inner_block(basis_block, basis_block), ROW_COL),
    )
    alpha_block = cross_sum / state_count
    alpha_square = jnp.dot(
        alpha_block.T, alpha_block, precision=highest, preferred_element_type=jnp.float32
    )
    basis_gram = basis_sum / state_count
    projected = jnp.dot(
        alpha_block.T,
        jnp.dot(basis_gram, alpha_block, precision=highest, preferred_element_type=jnp.float32),
        precision=highest,
        preferred_element_type=jnp.float32,
    )
    gram_block = image_sum / state_count - 2.0 * alpha_square + projected
    residual = applied - jnp.dot(
        alpha_block.T, basis_block, precision=highest, preferred_element_type=jnp.float32
    )
    lower_factor = jnp.linalg.cholesky(gram_block)
    basis_next = jax.scipy.linalg.solve_triangular(lower_factor, residual, lower=True)
    return (alpha_block, lower_factor.T, basis_next)


def solution(mesh):
    split = Mesh(mesh.devices.reshape(4, 2, 8, 8, 2), ("row_0", "row_1", "col_0", "col_1", "col_2"))
    in_specs = (
        P(None, ROW_COL),
        P(None, ROW_COL),
        P(),
        P(ROW_COL),
        P(ROW, COL, None, None, None),
        P(ROW, COL, None),
        P(ROW, COL, None),
        P(ROW, COL),
    )
    out_specs = (P(), P(), P(None, ROW_COL))
    return jax.shard_map(
        shards, mesh=split, in_specs=in_specs, out_specs=out_specs, check_vma=False
    )
```

profile of v0, /device:TPU:6, one launch (start us, length us, event | category | flops | bytes accessed | tf_op | source)
XLA Modules:
  0.0 343.7 jit_solution(23917158195824890)
XLA Ops:
  8.0 1.5 broadcast_in_dim.36
  9.5 10.0 %all-to-all-start = ((f32[8,1,32,128]{3,2,1,0:T(8,128)}), f32[8,1,32,128]{3,2,1,0:T(8,128)S(1)}, u32[]{:S(2)}, u32[]{:S(2)}) async-start(f32[8,1,32,128]{3,2,1,0:T(8,128)} %broadcast_in_dim.36), calls=%async_computation | async-start | bytes 262144 | tf_op jit(solution)/shard_map/all_to_all | solution.py:14
  19.5 0.0 reduce-scatter.4.cloned.1.call-start
  19.5 0.7 fusion.17
  20.2 0.7 compare_and_fusion.1
  21.5 0.7 fusion.18
  22.2 4.0 %all-to-all-done = f32[8,1,32,128]{3,2,1,0:T(8,128)S(1)} async-done(((f32[8,1,32,128]{3,2,1,0:T(8,128)}), f32[8,1,32,128]{3,2,1,0:T(8,128)S(1)}, u32[]{:S(2)}, u32[]{:S(2)}) %all-to-all-start) | async-done | bytes 131104 | tf_op jit(solution)/shard_map/all_to_all | solution.py:14
  26.2 0.6 gather_fusion
  26.8 1.8 convolution_multiply_fusion.1
  28.6 0.3 broadcast_in_dim.34
  28.8 1.2 scatter_fusion
  30.0 1.5 slice.20
  31.6 0.0 all-gather.3.cloned.1.call-start
  31.6 0.5 all-gather.3.cloned.1.call-update
  32.2 0.0 reduce-scatter.6.cloned.1.call-start
  32.2 53.3 %reduce-scatter.4.cloned.1.call-done = f32[16,32,128]{2,1,0:T(8,128)} async-done(((f32[128,32,128]{2,1,0:T(8,128)}), f32[16,32,128]{2,1,0:T(8,128)}) %reduce-scatter.4.cloned.1.call-update) | async-done | bytes 262160 | tf_op jit(solution)/shard_map/reduce_scatter | solution.py:30
  85.5 111.9 %all-gather.3.cloned.1.call-done = f32[4096,128]{1,0:T(8,128)} async-done(((f32[32,128]{1,0:T(8,128)}), f32[4096,128]{1,0:T(8,128)}) %all-gather.3.cloned.1.call-update) | async-done | bytes 2097168 | tf_op jit(solution)/shard_map/all_gather | solution.py:67
  197.5 2.2 gather_fusion.1
  199.6 1.0 convolution_multiply_fusion
  200.7 0.7 broadcast_in_dim.38
  201.3 2.4 scatter_fusion.1
  203.8 3.4 all-to-all-start.1
  207.1 0.0 reduce-scatter.8.cloned.1.call-start
  207.2 0.0 reduce-scatter.6.cloned.1.call-done
  207.2 0.7 reduce-scatter.8.cloned.1.call-update
  207.9 0.1 fusion.23
  208.0 5.8 %all-to-all-done.1 = f32[8,1,32,128]{3,2,1,0:T(8,128)S(1)} async-done(((f32[8,1,32,128]{3,2,1,0:T(8,128)}), f32[8,1,32,128]{3,2,1,0:T(8,128)S(1)}, u32[]{:S(2)}, u32[]{:S(2)}) %all-to-all-start.1) | async-done | bytes 131104 | tf_op jit(solution)/shard_map/all_to_all | solution.py:42
  213.8 18.5 %reduce-scatter.8.cloned.1.call-done = f32[1,32,128]{2,1,0:T(8,128)} async-done(((f32[2,32,128]{2,1,0:T(8,128)}), f32[1,32,128]{2,1,0:T(8,128)}) %reduce-scatter.8.cloned.1.call-update) | async-done | bytes 16400 | tf_op jit(solution)/shard_map/reduce_scatter | solution.py:30
  232.4 0.9 convolution_subtract_fusion.1
  233.2 0.1 convolution_bitcast_fusion
  233.4 0.1 fusion.22
  233.5 17.8 %all-reduce.2 = (f32[32,32]{0,1:T(8,128)S(1)}, f32[32,32]{0,1:T(8,128)S(1)}, f32[32,32]{0,1:T(8,128)S(1)}) all-reduce(f32[32,32]{0,1:T(8,128)S(1)} %convolution_bitcast_fusion, f32[32,32]{0,1:T(8,128)S(1)} %fusion.22, f32[32,32]{0,1:T(8,128)S(1)} %fusion.23), channel_id=1, replica_groups=mesh['row_0'=4,'row_1'=2,'col_0'=8,'col_1'=8,'col_2'=2] {'row_0'}, use_global_device_ids=true, to_apply=%region_6.7 | all-reduce | flops 3072 | bytes 24576 | tf_op jit(solution)/shard_map/psum | solution.py:48
  251.3 3.6 %all-reduce.4 = (f32[32,32]{0,1:T(8,128)S(1)}, f32[32,32]{0,1:T(8,128)S(1)}, f32[32,32]{0,1:T(8,128)S(1)}) all-reduce(f32[32,32]{0,1:T(8,128)S(1)} %get-tuple-element.15, f32[32,32]{0,1:T(8,128)S(1)} %get-tuple-element.16, f32[32,32]{0,1:T(8,128)S(1)} %get-tuple-element.17), channel_id=1, replica_groups=mesh['row_0'=4,'row_1'=2,'col_0'=8,'col_1'=8,'col_2'=2] {'row_1'}, use_global_device_ids=true, to_apply=%region_7.8 | all-reduce | flops 3072 | bytes 24576 | tf_op jit(solution)/shard_map/psum | solution.py:48
  254.9 30.4 %all-reduce.1 = (f32[32,32]{0,1:T(8,128)S(1)}, f32[32,32]{0,1:T(8,128)S(1)}, f32[32,32]{0,1:T(8,128)S(1)}) all-reduce(f32[32,32]{0,1:T(8,128)S(1)} %get-tuple-element.21, f32[32,32]{0,1:T(8,128)S(1)} %get-tuple-element.22, f32[32,32]{0,1:T(8,128)S(1)} %get-tuple-element.23), channel_id=1, replica_groups=mesh['row_0'=4,'row_1'=2,'col_0'=8,'col_1'=8,'col_2'=2] {'col_0'}, use_global_device_ids=true, to_apply=%region_8.9 | all-reduce | flops 3072 | bytes 24576 | tf_op jit(solution)/shard_map/psum | solution.py:48
  285.2 28.8 %all-reduce = (f32[32,32]{0,1:T(8,128)S(1)}, f32[32,32]{0,1:T(8,128)S(1)}, f32[32,32]{0,1:T(8,128)S(1)}) all-reduce(f32[32,32]{0,1:T(8,128)S(1)} %get-tuple-element.12, f32[32,32]{0,1:T(8,128)S(1)} %get-tuple-element.13, f32[32,32]{0,1:T(8,128)S(1)} %get-tuple-element.14), channel_id=1, replica_groups=mesh['row_0'=4,'row_1'=2,'col_0'=8,'col_1'=8,'col_2'=2] {'col_1'}, use_global_device_ids=true, to_apply=%region_9.10 | all-reduce | flops 3072 | bytes 24576 | tf_op jit(solution)/shard_map/psum | solution.py:48
  314.0 12.9 %all-reduce.3 = (f32[32,32]{0,1:T(8,128)S(1)}, f32[32,32]{0,1:T(8,128)S(1)}, f32[32,32]{0,1:T(8,128)S(1)}) all-reduce(f32[32,32]{0,1:T(8,128)S(1)} %get-tuple-element.9, f32[32,32]{0,1:T(8,128)S(1)} %get-tuple-element.10, f32[32,32]{0,1:T(8,128)S(1)} %get-tuple-element.11), channel_id=1, replica_groups=mesh['row_0'=4,'row_1'=2,'col_0'=8,'col_1'=8,'col_2'=2] {'col_2'}, use_global_device_ids=true, to_apply=%region_10.11 | all-reduce | flops 3072 | bytes 24576 | tf_op jit(solution)/shard_map/psum | solution.py:48
  326.9 0.1 convolution_subtract_fusion
  327.0 0.2 fusion.12
  327.2 0.2 fusion
  327.4 0.2 convolution_add_fusion
  327.6 0.1 copy.20
  327.7 2.9 cholesky.18
  330.6 0.6 compare_reduce_fusion
  331.3 0.7 select_bitcast_fusion
  331.9 2.4 custom-call.7
  334.4 0.7 copy.22
  335.1 0.7 copy.21
  335.8 0.8 fusion.9
  (24 shorter events, 0.2 us)
Async XLA Ops:
  8.0 18.8 %copy-start = (f32[1,1,16,128,128]{4,3,2,1,0:T(8,128)S(1)}, f32[1,1,16,128,128]{4,3,2,1,0:T(8,128)}, u32[]{:S(2)}) copy-start(f32[1,1,16,128,128]{4,3,2,1,0:T(8,128)} %param.12) | copy-start | bytes 3145732
  9.5 16.7 %all-to-all-start = ((f32[8,1,32,128]{3,2,1,0:T(8,128)}), f32[8,1,32,128]{3,2,1,0:T(8,128)S(1)}, u32[]{:S(2)}, u32[]{:S(2)}) async-start(f32[8,1,32,128]{3,2,1,0:T(8,128)} %broadcast_in_dim.36), calls=%async_computation | async-start | bytes 262144 | tf_op jit(solution)/shard_map/all_to_all | solution.py:14
  19.5 66.0 %reduce-scatter.4.cloned.1.call-start = ((), (), s32[]{:S(2)}) async-start(), calls=%async_computation.5 | async-start | bytes 2359296 | tf_op jit(solution)/shard_map/reduce_scatter | solution.py:30
  31.5 54.0 %copy-start.6 = (s32[1,1,16]{2,1,0:T(1,128)S(1)}, s32[1,1,16]{2,1,0:T(1,128)}, u32[]{:S(2)}) copy-start(s32[1,1,16]{2,1,0:T(1,128)} %param.13) | copy-start | bytes 196
  31.5 169.8 %copy-start.5 = (s32[1,1,16]{2,1,0:T(1,128)S(1)}, s32[1,1,16]{2,1,0:T(1,128)}, u32[]{:S(2)}) copy-start(s32[1,1,16]{2,1,0:T(1,128)} %param.14) | copy-start | bytes 196
  31.5 176.3 %copy-start.1 = (f32[32,128]{1,0:T(8,128)S(1)}, f32[32,128]{1,0:T(8,128)}, u32[]{:S(2)}) copy-start(f32[32,128]{1,0:T(8,128)} %param.8) | copy-start | bytes 49156
  31.5 200.8 %copy-start.2 = (f32[32,32]{1,0:T(8,128)S(1)}, f32[32,32]{1,0:T(8,128)}, u32[]{:S(2)}) copy-start(f32[32,32]{1,0:T(8,128)} %param.10) | copy-start | bytes 12292
  31.6 200.8 %copy-start.3 = (f32[32,128]{1,0:T(8,128)S(1)}, f32[32,128]{1,0:T(8,128)}, u32[]{:S(2)}) copy-start(f32[32,128]{1,0:T(8,128)} %param.9) | copy-start | bytes 49156
  31.6 200.8 %copy-start.4 = (f32[128]{0:T(128)S(1)}, f32[128]{0:T(128)}, u32[]{:S(2)}) copy-start(f32[128]{0:T(128)} %param.11) | copy-start | bytes 1540
  31.6 165.9 %all-gather.3.cloned.1.call-start = ((), (), s32[]{:S(2)}) async-start(), calls=%async_computation.8 | async-start | bytes 2113536 | tf_op jit(solution)/shard_map/all_gather | solution.py:67
  32.2 175.0 %reduce-scatter.6.cloned.1.call-start = ((), (), s32[]{:S(2)}) async-start(), calls=%async_computation.6 | async-start | bytes 294912 | tf_op jit(solution)/shard_map/reduce_scatter | solution.py:30
  203.8 10.1 %all-to-all-start.1 = ((f32[8,1,32,128]{3,2,1,0:T(8,128)}), f32[8,1,32,128]{3,2,1,0:T(8,128)S(1)}, u32[]{:S(2)}, u32[]{:S(2)}) async-start(f32[8,1,32,128]{3,2,1,0:T(8,128)} %bitcast.11), calls=%async_computation.4 | async-start | bytes 262144 | tf_op jit(solution)/shard_map/all_to_all | solution.py:42
  207.1 25.2 %reduce-scatter.8.cloned.1.call-start = ((), (), s32[]{:S(2)}) async-start(), calls=%async_computation.7 | async-start | bytes 49152 | tf_op jit(solution)/shard_map/reduce_scatter | solution.py:30
Sparse Core Ops, SparseCore 0:
  31.6 53.7 reduce-scatter.3
  88.8 41.5 reduce-scatter.5
  211.3 21.0 reduce-scatter.7
Sparse Core Ops, SparseCore 1:
  37.9 159.6 all-gather.2
where the time goes:
time: 345 us; the launch traced here: 344 us
  waiting for transfers between devices  195 us (57%)
  blocking collectives  93.3 us (27%)
  between operations  16.1 us (5%)
  starting transfers between devices  13.5 us (4%)
  other arithmetic  12.3 us (4%)
  local copies, waits for them, and re-layouts  8.05 us (2%)
  matrix products  5.63 us (2%)
    all_gather x1, waiting for transfers between devices, shards(): row_states = lax.all_gather(stacked, COL, axis=0, tiled=True)  112 us
    psum x5, blocking collectives, by_axis(): value = lax.psum(value, axis)  93.3 us
    reduce_scatter x3, waiting for transfers between devices, sum_by_axis(): subtotal = lax.psum_scatter(subtotal, axis, scatter_dimension=0, tiled=True)  71.8 us
    all_to_all x1, starting transfers between devices, from_everyone(): return lax.all_to_all(copies, axis, split_axis=0, concat_axis=0, tiled=True)  9.99 us
  transfers between devices with their start and end apart: 6, of which 5 were waited for; matrix products, arithmetic and copies ran while one was open for 2% of the time, Pallas kernels for 0%

commit v1 on v0

v1 whole, which is shorter than its diff:
```python
import functools

import jax
import jax.numpy as jnp
from jax import lax
from jax.experimental import pallas as pl
from jax.experimental.pallas import tpu as pltpu
from jax.sharding import Mesh
from jax.sharding import PartitionSpec as P

AXES = ("zl", "co", "y", "x", "zh")
ROW = ("zl", "co")
COL = ("y", "x", "zh")
K = 32
HALF = 16
LEN = 128
SLOTS = 16
RING = 8
MESH = pl.DeviceIdType.MESH
HIGHEST = lax.Precision.HIGHEST
NT = (((1,), (1,)), ((), ()))
NN = (((1,), (0,)), ((), ()))


def split(value):
    high = value.astype(jnp.bfloat16)
    low = (value - high.astype(jnp.float32)).astype(jnp.bfloat16)
    return high, low


def dot_three(left, right, dims):
    lh, ll = left
    rh, rl = right
    both = lax.dot_general(
        jnp.concatenate([lh, ll], axis=0), rh, dims, preferred_element_type=jnp.float32
    )
    rest = lax.dot_general(lh, rl, dims, preferred_element_type=jnp.float32)
    return both[:K] + (both[K:] + rest)


def exact_dot(left, right, dims):
    return lax.dot_general(
        left, right, dims, precision=HIGHEST, preferred_element_type=jnp.float32
    )


def remote(src, dst, send, recv, where):
    return pltpu.make_async_remote_copy(
        src_ref=src, dst_ref=dst, send_sem=send, recv_sem=recv, device_id=where, device_id_type=MESH
    )


def exchange_kernel(
    inv, rows, cols, count, basis, previous, coupling, energies, tiles_hbm,
    sums_out, applied_out,
    tiles, cstates, rstates, direct, part, ring_in, last, last_in, mid, z_in, msum, m_in, gram, core_in, dim_in,
    tile_sem,
    rg_s, rg_r, z0_s, z0_r, ex_s, ex_r, ag_s, ag_r, rs_s, rs_r, rx_s, rx_r, rz_s, rz_r, mr_s, mr_r,
    co_s, co_r, ar_s, ar_r,
):
    zl, co, y, x, zh = (lax.axis_index(a) for a in AXES)
    me_row = zl * 2 + co
    me_z = zh * 4 + zl
    zo = 1 - zh
    ring_pos = (y, x)
    exch_pos = (x, y)
    ring_axis = ("y", "x")
    exch_axis = ("x", "y")

    def row_id(r):
        return {"zl": r // 2, "co": r % 2}

    def z_id(z):
        return {"zh": z // 4, "zl": z % 4}

    tile_copy = pltpu.make_async_copy(tiles_hbm, tiles, tile_sem)
    tile_copy.start()

    barrier = pltpu.get_barrier_semaphore()

    def hello(where):
        pl.semaphore_signal(barrier, inc=1, device_id=where, device_id_type=MESH)

    for d in range(1, 8):
        hello({"x": (x + d) % 8})
        hello({"y": (y + d) % 8})
        hello(row_id((me_row + d) % 8))
    for d in range(4):
        hello({"zh": zo, "zl": (zl + d) % 4})
    for h in range(2):
        rstates[h, ring_pos[h], zh, exch_pos[h]] = basis[h * HALF : (h + 1) * HALF, :]
    cstates[me_row] = basis[...]
    direct[SLOTS] = jnp.zeros((K, LEN), jnp.float32)
    pl.semaphore_wait(barrier, 25)

    sends = []

    def go(copy):
        copy.start()
        sends.append(copy)

    for h in range(2):
        slot = rstates.at[h, ring_pos[h], zh, exch_pos[h]]
        go(remote(basis.at[pl.ds(h * HALF, HALF)], slot, z0_s.at[h], z0_r.at[h], {"zh": zo}))
    for d in (4, 3, 5, 2, 6, 1, 7):
        for h in range(2):
            slot = rstates.at[h, ring_pos[h], zh, exch_pos[h]]
            go(
                remote(
                    basis.at[pl.ds(h * HALF, HALF)], slot, ex_s.at[h, 0, d], ex_r.at[h, 0, d],
                    {exch_axis[h]: (exch_pos[h] + d) % 8},
                )
            )
    for d in range(1, 8):
        go(remote(basis, cstates.at[me_row], rg_s.at[d], rg_r.at[d], row_id((me_row + d) % 8)))

    def exch_wait(h, c):
        zc = (zh, zo)[c]
        for d in range(1, 8):
            slot = rstates.at[h, ring_pos[h], zc, (exch_pos[h] + 8 - d) % 8]
            remote(slot, slot, ex_s.at[h, c, d], ex_r.at[h, c, d], {exch_axis[h]: exch_pos[h]}).wait_recv()

    def hops(sign, c):
        return 4 if (sign > 0) == (c == 0) else 3

    def ag_copy(h, g, c, s):
        sign = (1, -1)[g]
        zc = (zh, zo)[c]
        slot = rstates.at[h, (ring_pos[h] + 8 - sign * (s - 1)) % 8, zc]
        return remote(
            slot, slot, ag_s.at[h, g, c, s - 1], ag_r.at[h, g, c, s - 1],
            {ring_axis[h]: (ring_pos[h] + 8 + sign) % 8},
        )

    def ag_wait(h, g, c, s):
        sign = (1, -1)[g]
        zc = (zh, zo)[c]
        slot = rstates.at[h, (ring_pos[h] + 8 - sign * s) % 8, zc]
        remote(
            slot, slot, ag_s.at[h, g, c, s - 1], ag_r.at[h, g, c, s - 1],
            {ring_axis[h]: (ring_pos[h] + 8 + sign) % 8},
        ).wait_recv()

    for h in range(2):
        slot = rstates.at[h, ring_pos[h], zo, exch_pos[h]]
        remote(slot, slot, z0_s.at[h], z0_r.at[h], {"zh": zo}).wait_recv()
        for d in (4, 3, 5, 2, 6, 1, 7):
            go(
                remote(
                    slot, slot, ex_s.at[h, 1, d], ex_r.at[h, 1, d],
                    {exch_axis[h]: (exch_pos[h] + d) % 8},
                )
            )
    for h in range(2):
        exch_wait(h, 0)
        for g in range(2):
            go(ag_copy(h, g, 0, 1))

    for d in range(1, 8):
        slot = cstates.at[(me_row + 8 - d) % 8]
        remote(slot, slot, rg_s.at[d], rg_r.at[d], row_id(me_row)).wait_recv()
    tile_copy.wait()
    for s in range(SLOTS):
        direct[s] = dot_three(split(cstates[cols[s]]), split(tiles[s]), NT)
    for h in range(2):
        exch_wait(h, 1)
        for g in range(2):
            go(ag_copy(h, g, 1, 1))

    for a in range(8):
        for b in range(8):
            for z in range(2):
                value = direct[inv[(a * 8 + b) * 2 + z]]
                part[0, a, z, b] = value[:HALF]
                part[1, b, z, a] = value[HALF:]

    def rs_copy(h, g, c, s):
        sign = (1, -1)[g]
        zc = (zo, zh)[c]
        slot = part.at[h, (ring_pos[h] + 8 + sign * (5 - s)) % 8, zc]
        return remote(
            slot, ring_in.at[h, g, c, s - 1], rs_s.at[h, g, c, s - 1], rs_r.at[h, g, c, s - 1],
            {ring_axis[h]: (ring_pos[h] + 8 + sign) % 8},
        )

    def rs_wait(h, g, c, s):
        slot = ring_in.at[h, g, c, s - 1]
        sign = (1, -1)[g]
        remote(
            slot, slot, rs_s.at[h, g, c, s - 1], rs_r.at[h, g, c, s - 1],
            {ring_axis[h]: (ring_pos[h] + 8 + sign) % 8},
        ).wait_recv()

    for c in range(2):
        for h in range(2):
            for g in range(2):
                if hops((1, -1)[g], c) == 4:
                    go(rs_copy(h, g, c, 1))
    for s in range(1, 5):
        for c in range(2):
            for h in range(2):
                for g in range(2):
                    sign = (1, -1)[g]
                    n = hops(sign, c)
                    if s <= n:
                        ag_wait(h, g, c, s)
                        if s < n:
                            go(ag_copy(h, g, c, s + 1))
        for c in range(2):
            zc = (zo, zh)[c]
            for h in range(2):
                for g in range(2):
                    sign = (1, -1)[g]
                    n = hops(sign, c)
                    if n == 4 or s > 1:
                        rs_wait(h, g, c, s)
                    if s < 4:
                        to = (ring_pos[h] + 8 + sign * (4 - s)) % 8
                        if n == 4 or s > 1:
                            part[h, to, zc] = part[h, to, zc] + ring_in[h, g, c, s - 1]
                        go(rs_copy(h, g, c, s + 1))
    for c in range(2):
        zc = (zo, zh)[c]
        for h in range(2):
            last[h, c] = part[h, ring_pos[h], zc] + (ring_in[h, 0, c, 3] + ring_in[h, 1, c, 3])
            for d in (4, 3, 5, 2, 6, 1, 7):
                to = (exch_pos[h] + d) % 8
                go(
                    remote(
                        last.at[h, c, to], last_in.at[h, c, d], rx_s.at[h, c, d], rx_r.at[h, c, d],
                        {exch_axis[h]: to},
                    )
                )

    mirror = []
    for s in range(SLOTS):
        t = rows[s]
        at_y, at_x, at_z = t // 16, (t // 2) % 8, t % 2
        picked = jnp.concatenate([rstates[0, at_y, at_z, at_x], rstates[1, at_x, at_z, at_y]], axis=0)
        mirror.append(dot_three(split(picked), split(tiles[s]), NN))
    live = count[0]
    for u in range(8):
        total = jnp.zeros((K, LEN), jnp.float32)
        for s in range(SLOTS):
            weight = jnp.where((cols[s] == u) & (s < live), 1.0, 0.0)
            total = total + weight * mirror[s]
        msum[u] = total
    for d in (4, 3, 5, 2, 6, 1, 7):
        to = (me_row + d) % 8
        go(remote(msum.at[to], m_in.at[d], mr_s.at[d], mr_r.at[d], row_id(to)))

    halves = []
    for c in range(2):
        for h in range(2):
            total = last[h, c, exch_pos[h]]
            for d in range(1, 8):
                slot = last_in.at[h, c, d]
                remote(slot, slot, rx_s.at[h, c, d], rx_r.at[h, c, d], {exch_axis[h]: exch_pos[h]}).wait_recv()
                total = total + last_in[h, c, d]
            if c == 0:
                mid[h] = total
                go(remote(mid.at[h], z_in.at[h], rz_s.at[h], rz_r.at[h], {"zh": zo}))
            else:
                halves.append(total)
    own_mirror = msum[me_row]
    for d in range(1, 8):
        slot = m_in.at[d]
        remote(slot, slot, mr_s.at[d], mr_r.at[d], row_id(me_row)).wait_recv()
        own_mirror = own_mirror + m_in[d]
    vectors = basis[...]
    applied = energies[...] * vectors + own_mirror - exact_dot(coupling[...], previous[...], NN)
    for h in range(2):
        slot = z_in.at[h]
        remote(slot, slot, rz_s.at[h], rz_r.at[h], {"zh": zo}).wait_recv()
    applied = applied + jnp.concatenate([halves[0] + z_in[0], halves[1] + z_in[1]], axis=0)
    applied_out[...] = applied

    zero = jnp.zeros((K, LEN), jnp.float32)
    total = exact_dot(vectors, jnp.concatenate([applied, zero, vectors, zero], axis=0), NT)
    total = total + exact_dot(applied, jnp.concatenate([zero, applied, zero, zero], axis=0), NT)
    gram[0] = total
    go(remote(gram.at[0], core_in, co_s, co_r, {"co": 1 - co}))
    remote(core_in, core_in, co_s, co_r, {"co": 1 - co}).wait_recv()
    total = total + core_in[...]
    for dim in range(3):
        gram[1 + dim] = total
        for d in (4, 3, 5, 2, 6, 1, 7):
            where = ({"x": (x + d) % 8}, {"y": (y + d) % 8}, z_id((me_z + d) % 8))[dim]
            go(remote(gram.at[1 + dim], dim_in.at[dim, d], ar_s.at[dim, d], ar_r.at[dim, d], where))
        for d in (1, 7, 2, 6, 3, 5, 4):
            slot = dim_in.at[dim, d]
            remote(slot, slot, ar_s.at[dim, d], ar_r.at[dim, d], {"x": x}).wait_recv()
        here = (x, y, me_z)[dim]
        dim_in[dim, 0] = total
        total = dim_in[dim, here]
        for k in range(1, 8):
            total = total + dim_in[dim, (here + 8 - k) % 8]
    sums_out[...] = total
    for copy in sends:
        copy.wait_send()


def finish_kernel(state_count, sums, basis, applied, alpha_out, beta_out, next_out):
    scaled = sums[...] * (1.0 / state_count)
    alpha = scaled[:, :K]
    image = scaled[:, K : 2 * K]
    basis_gram = scaled[:, 2 * K : 3 * K]
    alpha_out[...] = alpha
    alpha_t = alpha.T
    square = exact_dot(alpha_t, alpha, NN)
    projected = exact_dot(alpha_t, exact_dot(basis_gram, alpha, NN), NN)
    gram = image - 2.0 * square + projected
    residual = applied[...] - exact_dot(alpha_t, basis[...], NN)
    at_row = lax.broadcasted_iota(jnp.int32, (K, K), 0)
    at_col = lax.broadcasted_iota(jnp.int32, (K, K), 1)
    eye = jnp.where(at_row == at_col, 1.0, 0.0)
    work = jnp.concatenate([gram, eye], axis=1)
    index = lax.broadcasted_iota(jnp.int32, (K, 2 * K), 0)
    for j in range(K):
        pivot_row = work[j : j + 1, :]
        pivot = work[j : j + 1, j : j + 1]
        scale = 1.0 / jnp.sqrt(pivot)
        row = pivot_row * scale
        column = work[:, j : j + 1] * scale
        work = jnp.where(index > j, work - column * row, jnp.where(index == j, row, work))
    beta_out[...] = jnp.where(at_row <= at_col, work[:, :K], 0.0)
    next_out[...] = exact_dot(work[:, K:], residual, NN)


def shards(basis, previous, coupling, energies, tile_values, tile_rows, tile_cols, counts):
    state_count = basis.shape[1] * lax.axis_size(ROW) * lax.axis_size(COL)
    tiles = tile_values.reshape(SLOTS, LEN, LEN)
    rows = tile_rows.reshape(SLOTS)
    cols = tile_cols.reshape(SLOTS)
    count = counts.reshape(1)
    slot = jnp.arange(SLOTS, dtype=jnp.int32)
    hit = (rows[:, None] == jnp.arange(LEN, dtype=jnp.int32)[None, :]) & (slot < count)[:, None]
    inv = jnp.min(jnp.where(hit, slot[:, None], SLOTS), axis=0)
    f32 = jnp.float32
    vmem = pl.BlockSpec(memory_space=pltpu.VMEM)
    smem = pl.BlockSpec(memory_space=pltpu.SMEM)
    dma = pltpu.SemaphoreType.DMA
    sums, applied = pl.pallas_call(
        exchange_kernel,
        out_shape=(jax.ShapeDtypeStruct((K, LEN), f32), jax.ShapeDtypeStruct((K, LEN), f32)),
        in_specs=[smem, smem, smem, smem, vmem, vmem, vmem, vmem, pl.BlockSpec(memory_space=pl.ANY)],
        out_specs=(vmem, vmem),
        scratch_shapes=[
            pltpu.VMEM((SLOTS, LEN, LEN), f32),
            pltpu.VMEM((8, K, LEN), f32),
            pltpu.VMEM((2, 8, 2, 8, HALF, LEN), f32),
            pltpu.VMEM((SLOTS + 1, K, LEN), f32),
            pltpu.VMEM((2, 8, 2, 8, HALF, LEN), f32),
            pltpu.VMEM((2, 2, 2, 4, 8, HALF, LEN), f32),
            pltpu.VMEM((2, 2, 8, HALF, LEN), f32),
            pltpu.VMEM((2, 2, 8, HALF, LEN), f32),
            pltpu.VMEM((2, HALF, LEN), f32),
            pltpu.VMEM((2, HALF, LEN), f32),
            pltpu.VMEM((8, K, LEN), f32),
            pltpu.VMEM((8, K, LEN), f32),
            pltpu.VMEM((4, K, LEN), f32),
            pltpu.VMEM((K, LEN), f32),
            pltpu.VMEM((3, 8, K, LEN), f32),
            dma(()),
            dma((8,)), dma((8,)),
            dma((2,)), dma((2,)),
            dma((2, 2, 8)), dma((2, 2, 8)),
            dma((2, 2, 2, 4)), dma((2, 2, 2, 4)),
            dma((2, 2, 2, 4)), dma((2, 2, 2, 4)),
            dma((2, 2, 8)), dma((2, 2, 8)),
            dma((2,)), dma((2,)),
            dma((8,)), dma((8,)),
            dma(()), dma(()),
            dma((3, 8)), dma((3, 8)),
        ],
        compiler_params=pltpu.CompilerParams(
            collective_id=0, has_side_effects=True, vmem_limit_bytes=40 * 1024 * 1024
        ),
        name="exchange",
    )(inv, rows, cols, count, basis, previous, coupling, energies.reshape(1, LEN), tiles)
    return pl.pallas_call(
        functools.partial(finish_kernel, state_count),
        out_shape=(
            jax.ShapeDtypeStruct((K, K), f32),
            jax.ShapeDtypeStruct((K, K), f32),
            jax.ShapeDtypeStruct((K, LEN), f32),
        ),
        in_specs=[vmem] * 3,
        out_specs=(vmem, vmem, vmem),
        name="finish",
    )(sums, basis, applied)


def solution(mesh):
    split_mesh = Mesh(mesh.devices.reshape(4, 2, 8, 8, 2), AXES)
    both = ROW + COL
    in_specs = (
        P(None, both),
        P(None, both),
        P(),
        P(both),
        P(ROW, COL, None, None, None),
        P(ROW, COL, None),
        P(ROW, COL, None),
        P(ROW, COL),
    )
    out_specs = (P(), P(), P(None, both))
    return jax.shard_map(
        shards, mesh=split_mesh, in_specs=in_specs, out_specs=out_specs, check_vma=False
    )
```

time: 345 us -> 95.5 us (0.28)
  the two profiles are of different devices: /device:TPU:6 before, /device:TPU:1 now
where the time goes in v1:
time: 95.5 us; the launch traced here: 94.9 us
  Pallas kernels  88.2 us (92%)
  local copies, waits for them, and re-layouts  4.51 us (5%)
  between operations  1.37 us (1%)
    pallas_call x1, Pallas kernels, shards(): pl.pallas_call(exchange_kernel, out_shape=(jax.ShapeDtypeStruct((K, LEN),...  83.1 us
    pallas_call x1, Pallas kernels, shards(): pl.pallas_call(functools.partial(finish_kernel, state_count), out_shape=(...  5.14 us
    unnamed x18, local copies, waits for them, and re-layouts  4.51 us

profile of v1, /device:TPU:1, one launch (start us, length us, event | category | flops | bytes accessed | tf_op | source)
XLA Modules:
  0.0 94.9 jit_solution(15081788479832991923)
XLA Ops:
  0.6 0.0 copy-start.1
  1.3 0.0 copy-start.6
  1.3 0.0 copy-start.7
  1.3 0.8 select_reduce_fusion.inv
  2.1 0.0 copy-done.1
  2.1 0.0 copy-done.6
  2.1 0.0 copy-done.7
  2.2 0.0 copy-start
  2.2 1.2 %copy-done = f32[1,1,16,128,128]{4,3,2,1,0:T(8,128)S(1)} copy-done((f32[1,1,16,128,128]{4,3,2,1,0:T(8,128)S(1)}, f32[1,1,16,128,128]{4,3,2,1,0:T(8,128)}, u32[]{:S(2)}) %copy-start) | copy-done | bytes 1048600
  3.4 0.0 copy-start.2
  3.4 0.7 copy-done.2
  4.1 0.0 copy-start.3
  4.1 0.7 copy-done.3
  4.8 0.0 copy-start.8
  4.8 0.7 copy-done.8
  5.5 83.1 %exchange.1 = (f32[32,128]{1,0:T(8,128)S(1)}, f32[32,128]{1,0:T(8,128)S(1)}) custom-call(s32[128]{0:T(128)S(1)} %select_reduce_fusion.inv, s32[16]{0:T(128)S(1)} %bitcast.10, s32[16]{0:T(128)S(1)} %bitcast.11, s32[1]{0:T(128)} %bitcast.7.count, f32[32,128]{1,0:T(8,128)S(1)} %copy-done.1, f32[32,128]{1,0:T(8,128)S(1)} %copy-done.2, f32[32,32]{1,0:T(8,128)S(1)} %copy-done.3, ...), custom_call_target="tpu_custom_call" | custom-call | tf_op jit(solution)/shard_map/exchange/pallas_call | solution.py:343
  88.6 0.0 copy-start.4
  88.6 0.6 copy-done.4
  89.2 0.0 copy-start.5
  89.2 0.6 copy-done.5
  89.8 5.1 %finish.1 = (f32[32,32]{1,0:T(8,128)}, f32[32,32]{1,0:T(8,128)}, f32[32,128]{1,0:T(8,128)}) custom-call(f32[32,128]{1,0:T(8,128)} %copy-done.4, f32[32,128]{1,0:T(8,128)} %basis.3, f32[32,128]{1,0:T(8,128)} %copy-done.5), custom_call_target="tpu_custom_call" | custom-call | tf_op jit(solution)/shard_map/finish/pallas_call | solution.py:381
  (1 shorter events, 0.0 us)
Async XLA Ops:
  0.6 1.5 %copy-start.1 = (f32[32,128]{1,0:T(8,128)S(1)}, f32[32,128]{1,0:T(8,128)}, u32[]{:S(2)}) copy-start(f32[32,128]{1,0:T(8,128)} %basis.3) | copy-start | bytes 49156
  1.3 0.8 copy-start.6
  1.3 0.8 copy-start.7
  2.2 1.2 %copy-start = (f32[1,1,16,128,128]{4,3,2,1,0:T(8,128)S(1)}, f32[1,1,16,128,128]{4,3,2,1,0:T(8,128)}, u32[]{:S(2)}) copy-start(f32[1,1,16,128,128]{4,3,2,1,0:T(8,128)} %param.12) | copy-start | bytes 3145732
  3.4 0.7 copy-start.2
  4.1 0.7 copy-start.3
  4.8 0.7 copy-start.8
  88.6 0.6 copy-start.4
  89.2 0.6 copy-start.5

commit v2 on v1

v2 whole, which is shorter than its diff:
```python
import functools

import jax
import jax.numpy as jnp
from jax import lax
from jax.experimental import pallas as pl
from jax.experimental.pallas import tpu as pltpu
from jax.sharding import Mesh
from jax.sharding import PartitionSpec as P

AXES = ("zl", "co", "y", "x", "zh")
ROW = ("zl", "co")
COL = ("y", "x", "zh")
K = 32
HALF = 16
LEN = 128
SLOTS = 16
VMEM_LIMIT = 64 * 1024 * 1024 - 65536
RING = 8
MESH = pl.DeviceIdType.MESH
HIGHEST = lax.Precision.HIGHEST
NT = (((1,), (1,)), ((), ()))
NN = (((1,), (0,)), ((), ()))


def split(value):
    high = value.astype(jnp.bfloat16)
    low = (value - high.astype(jnp.float32)).astype(jnp.bfloat16)
    return high, low


def dot_three(left, right, dims):
    lh, ll = left
    rh, rl = right
    both = lax.dot_general(
        jnp.concatenate([lh, ll], axis=0), rh, dims, preferred_element_type=jnp.float32
    )
    rest = lax.dot_general(lh, rl, dims, preferred_element_type=jnp.float32)
    return both[:K] + (both[K:] + rest)


def exact_dot(left, right, dims):
    return lax.dot_general(
        left, right, dims, precision=HIGHEST, preferred_element_type=jnp.float32
    )


def remote(src, dst, send, recv, where):
    return pltpu.make_async_remote_copy(
        src_ref=src, dst_ref=dst, send_sem=send, recv_sem=recv, device_id=where, device_id_type=MESH
    )


def pack(block):
    out = block[:8]
    for q in range(1, 4):
        out = out + pltpu.roll(block[8 * q : 8 * q + 8], 32 * q, 1)
    return out


def unpack(block):
    return jnp.concatenate([block[:, 32 * q : 32 * q + 32] for q in range(4)], axis=0)


def wide(block):
    return jnp.concatenate([block, jnp.zeros((K, LEN - K), jnp.float32)], axis=1)


def finish(state_count, alpha_sum, basis_sum, image_sum, vectors, applied, alpha_out, beta_out, next_out):
    alpha = alpha_sum * (1.0 / state_count)
    basis_gram = basis_sum * (1.0 / state_count)
    alpha_t = alpha.T
    square = exact_dot(alpha_t, alpha, NN)
    projected = exact_dot(alpha_t, exact_dot(basis_gram, alpha, NN), NN)
    residual = applied - exact_dot(alpha_t, vectors, NN)
    alpha_out[...] = alpha
    gram = image_sum() * (1.0 / state_count) - 2.0 * square + projected
    at_row = lax.broadcasted_iota(jnp.int32, (K, K), 0)
    at_col = lax.broadcasted_iota(jnp.int32, (K, K), 1)
    eye = jnp.where(at_row == at_col, 1.0, 0.0)
    work = jnp.concatenate([gram, eye], axis=1)
    index = lax.broadcasted_iota(jnp.int32, (K, 2 * K), 0)
    for j in range(K):
        scale = 1.0 / jnp.sqrt(work[j : j + 1, j : j + 1])
        row = work[j : j + 1, :] * scale
        column = work[:, j : j + 1] * scale
        work = jnp.where(index > j, work - column * row, jnp.where(index == j, row, work))
    beta_out[...] = jnp.where(at_row <= at_col, work[:, :K], 0.0)
    next_out[...] = exact_dot(work[:, K:], residual, NN)


def exchange_kernel(
    state_count,
    rows_hbm, cols_hbm, count_hbm, basis_hbm, previous_hbm, coupling_hbm, energies_hbm, tiles_hbm,
    alpha_out, beta_out, next_out,
    rows, cols, count, inv, inv_lanes, basis, previous, coupling, energies,
    tiles, cstates, rstates, direct, part, ring_in, last, last_in, mid, z_in, msum, m_in,
    early, early_in, early_dim, late, late_in, late_dim,
    in_sem, inv_sem,
    rg_s, rg_r, z0_s, z0_r, ex_s, ex_r, ag_s, ag_r, rs_s, rs_r, rx_s, rx_r, rz_s, rz_r, mr_s, mr_r,
    ec_s, ec_r, er_s, er_r, lc_s, lc_r, lr_s, lr_r,
):
    zl, co, y, x, zh = (lax.axis_index(a) for a in AXES)
    me_row = zl * 2 + co
    me_z = zh * 4 + zl
    zo = 1 - zh
    ring_pos = (y, x)
    exch_pos = (x, y)
    ring_axis = ("y", "x")
    exch_axis = ("x", "y")
    order = (4, 3, 5, 2, 6, 1, 7)

    def row_id(r):
        return {"zl": r // 2, "co": r % 2}

    def z_id(z):
        return {"zh": z // 4, "zl": z % 4}

    barrier = pltpu.get_barrier_semaphore()

    def hello(where):
        pl.semaphore_signal(barrier, inc=1, device_id=where, device_id_type=MESH)

    for d in order:
        hello({"x": (x + d) % 8})
        hello({"y": (y + d) % 8})
        hello(row_id((me_row + d) % 8))
    for d in range(4):
        hello({"zh": zo, "zl": (zl + d) % 4})

    loads = [
        pltpu.make_async_copy(src, dst, in_sem.at[i])
        for i, (src, dst) in enumerate(
            (
                (basis_hbm, basis), (rows_hbm, rows), (count_hbm, count), (cols_hbm, cols), (tiles_hbm, tiles),
                (previous_hbm, previous), (coupling_hbm, coupling), (energies_hbm, energies),
            )
        )
    ]
    for copy in loads:
        copy.start()
    direct[SLOTS] = jnp.zeros((K, LEN), jnp.float32)
    loads[0].wait()
    for h in range(2):
        rstates[h, ring_pos[h], zh, exch_pos[h]] = basis[h * HALF : (h + 1) * HALF, :]
    cstates[me_row] = basis[...]
    loads[1].wait()
    loads[2].wait()
    live = count[0, 0]
    lane = lax.broadcasted_iota(jnp.int32, (8, LEN), 1)
    table = jnp.full((8, LEN), SLOTS, jnp.int32)
    for s in range(SLOTS):
        table = jnp.where(lane == jnp.where(s < live, rows[s], -1), s, table)
    inv_lanes[...] = table
    inv_copy = pltpu.make_async_copy(inv_lanes.at[pl.ds(0, 1)], inv, inv_sem)
    inv_copy.start()
    pl.semaphore_wait(barrier, 25)

    sends = []

    def go(copy):
        copy.start()
        sends.append(copy)

    for h in range(2):
        slot = rstates.at[h, ring_pos[h], zh, exch_pos[h]]
        go(remote(basis.at[pl.ds(h * HALF, HALF)], slot, z0_s.at[h], z0_r.at[h], {"zh": zo}))
    for d in order:
        for h in range(2):
            slot = rstates.at[h, ring_pos[h], zh, exch_pos[h]]
            go(
                remote(
                    basis.at[pl.ds(h * HALF, HALF)], slot, ex_s.at[h, 0, d], ex_r.at[h, 0, d],
                    {exch_axis[h]: (exch_pos[h] + d) % 8},
                )
            )
        go(remote(basis, cstates.at[me_row], rg_s.at[d], rg_r.at[d], row_id((me_row + d) % 8)))

    def exch_wait(h, c):
        zc = (zh, zo)[c]
        for d in range(1, 8):
            slot = rstates.at[h, ring_pos[h], zc, (exch_pos[h] + 8 - d) % 8]
            remote(slot, slot, ex_s.at[h, c, d], ex_r.at[h, c, d], {exch_axis[h]: exch_pos[h]}).wait_recv()

    def hops(sign, c):
        return 4 if (sign > 0) == (c == 0) else 3

    def ag_copy(h, g, c, s):
        sign = (1, -1)[g]
        zc = (zh, zo)[c]
        slot = rstates.at[h, (ring_pos[h] + 8 - sign * (s - 1)) % 8, zc]
        return remote(
            slot, slot, ag_s.at[h, g, c, s - 1], ag_r.at[h, g, c, s - 1],
            {ring_axis[h]: (ring_pos[h] + 8 + sign) % 8},
        )

    def ag_wait(h, g, c, s):
        sign = (1, -1)[g]
        zc = (zh, zo)[c]
        slot = rstates.at[h, (ring_pos[h] + 8 - sign * s) % 8, zc]
        remote(
            slot, slot, ag_s.at[h, g, c, s - 1], ag_r.at[h, g, c, s - 1],
            {ring_axis[h]: (ring_pos[h] + 8 + sign) % 8},
        ).wait_recv()

    for h in range(2):
        slot = rstates.at[h, ring_pos[h], zo, exch_pos[h]]
        remote(slot, slot, z0_s.at[h], z0_r.at[h], {"zh": zo}).wait_recv()
        for d in order:
            go(
                remote(
                    slot, slot, ex_s.at[h, 1, d], ex_r.at[h, 1, d],
                    {exch_axis[h]: (exch_pos[h] + d) % 8},
                )
            )
    for h in range(2):
        exch_wait(h, 0)
        for g in range(2):
            go(ag_copy(h, g, 0, 1))

    for d in range(1, 8):
        slot = cstates.at[(me_row + 8 - d) % 8]
        remote(slot, slot, rg_s.at[d], rg_r.at[d], row_id(me_row)).wait_recv()
    for copy in loads[3:]:
        copy.wait()
    inv_copy.wait()
    for s in range(SLOTS):
        direct[s] = dot_three(split(cstates[cols[s]]), split(tiles[s]), NT)
    for h in range(2):
        exch_wait(h, 1)
        for g in range(2):
            go(ag_copy(h, g, 1, 1))

    for a in range(8):
        for b in range(8):
            for z in range(2):
                value = direct[inv[0, (a * 8 + b) * 2 + z]]
                part[0, a, z, b] = value[:HALF]
                part[1, b, z, a] = value[HALF:]

    def rs_copy(h, g, c, s):
        sign = (1, -1)[g]
        zc = (zo, zh)[c]
        slot = part.at[h, (ring_pos[h] + 8 + sign * (5 - s)) % 8, zc]
        return remote(
            slot, ring_in.at[h, g, c, s - 1], rs_s.at[h, g, c, s - 1], rs_r.at[h, g, c, s - 1],
            {ring_axis[h]: (ring_pos[h] + 8 + sign) % 8},
        )

    def rs_wait(h, g, c, s):
        slot = ring_in.at[h, g, c, s - 1]
        sign = (1, -1)[g]
        remote(
            slot, slot, rs_s.at[h, g, c, s - 1], rs_r.at[h, g, c, s - 1],
            {ring_axis[h]: (ring_pos[h] + 8 + sign) % 8},
        ).wait_recv()

    def rs_step(c, s):
        zc = (zo, zh)[c]
        for h in range(2):
            for g in range(2):
                sign = (1, -1)[g]
                n = hops(sign, c)
                if s == 0:
                    if n == 4:
                        go(rs_copy(h, g, c, 1))
                    continue
                if n == 4 or s > 1:
                    rs_wait(h, g, c, s)
                if s < 4:
                    to = (ring_pos[h] + 8 + sign * (4 - s)) % 8
                    if n == 4 or s > 1:
                        part[h, to, zc] = part[h, to, zc] + ring_in[h, g, c, s - 1]
                    go(rs_copy(h, g, c, s + 1))

    def rs_last(c):
        zc = (zo, zh)[c]
        for h in range(2):
            last[h, c] = part[h, ring_pos[h], zc] + (ring_in[h, 0, c, 3] + ring_in[h, 1, c, 3])
            for d in order:
                to = (exch_pos[h] + d) % 8
                go(
                    remote(
                        last.at[h, c, to], last_in.at[h, c, d], rx_s.at[h, c, d], rx_r.at[h, c, d],
                        {exch_axis[h]: to},
                    )
                )

    def ag_step(s):
        for c in range(2):
            for h in range(2):
                for g in range(2):
                    n = hops((1, -1)[g], c)
                    if s <= n:
                        ag_wait(h, g, c, s)
                        if s < n:
                            go(ag_copy(h, g, c, s + 1))

    rs_step(0, 0)
    for s in range(1, 5):
        ag_step(s)
        rs_step(1, s - 1)
        rs_step(0, s)
    rs_last(0)
    rs_step(1, 4)
    rs_last(1)

    mirror = []
    row_parts = []
    for s in range(SLOTS):
        t = rows[s]
        at_y, at_x, at_z = t // 16, (t // 2) % 8, t % 2
        picked = split(
            jnp.concatenate([rstates[0, at_y, at_z, at_x], rstates[1, at_x, at_z, at_y]], axis=0)
        )
        row_parts.append(picked)
        mirror.append(dot_three(picked, split(tiles[s]), NN))
    for u in range(8):
        total = jnp.zeros((K, LEN), jnp.float32)
        for s in range(SLOTS):
            weight = jnp.where((cols[s] == u) & (s < live), 1.0, 0.0)
            total = total + weight * mirror[s]
        msum[u] = total
    for d in order:
        to = (me_row + d) % 8
        go(remote(msum.at[to], m_in.at[d], mr_s.at[d], mr_r.at[d], row_id(to)))

    vectors = basis[...]
    own = energies[...] * vectors - exact_dot(coupling[...], previous[...], NN)
    live_direct = [split(jnp.where(s < live, 1.0, 0.0) * direct[s]) for s in range(SLOTS)]
    rh = jnp.concatenate([p[0] for p in row_parts], axis=1)
    rl = jnp.concatenate([p[1] for p in row_parts], axis=1)
    dh = jnp.concatenate([p[0] for p in live_direct], axis=1)
    dl = jnp.concatenate([p[1] for p in live_direct], axis=1)
    cross = lax.dot_general(jnp.concatenate([rh, rl], axis=0), dh, NT, preferred_element_type=jnp.float32)
    cross = cross[:K] + (cross[K:] + lax.dot_general(rh, dl, NT, preferred_element_type=jnp.float32))
    cross = cross + cross.T + exact_dot(vectors, own, NT)
    early[0, :8] = pack(wide(cross))
    early[0, 8:] = pack(wide(exact_dot(vectors, vectors, NT)))

    def core_start(src, dst, send, recv):
        go(remote(src, dst, send, recv, {"co": 1 - co}))

    def core_wait(dst, send, recv):
        remote(dst, dst, send, recv, {"co": 1 - co}).wait_recv()

    def dim_start(dim, src, dst, send, recv):
        for d in order:
            where = ({"x": (x + d) % 8}, {"y": (y + d) % 8}, z_id((me_z + d) % 8))[dim]
            go(remote(src, dst.at[dim, d], send.at[dim, d], recv.at[dim, d], where))

    def dim_wait(dim, mine, dst, send, recv):
        for d in range(1, 8):
            slot = dst.at[dim, d]
            remote(slot, slot, send.at[dim, d], recv.at[dim, d], {"x": x}).wait_recv()
        dst[dim, 0] = mine
        here = (x, y, me_z)[dim]
        total = dst[dim, here]
        for k in range(1, 8):
            total = total + dst[dim, (here + 8 - k) % 8]
        return total

    core_start(early.at[0], early_in, ec_s, ec_r)

    halves = []
    for c in range(2):
        for h in range(2):
            total = last[h, c, exch_pos[h]]
            for d in range(1, 8):
                slot = last_in.at[h, c, d]
                remote(slot, slot, rx_s.at[h, c, d], rx_r.at[h, c, d], {exch_axis[h]: exch_pos[h]}).wait_recv()
                total = total + last_in[h, c, d]
            if c == 0:
                mid[h] = total
                go(remote(mid.at[h], z_in.at[h], rz_s.at[h], rz_r.at[h], {"zh": zo}))
            else:
                halves.append(total)
    core_wait(early_in, ec_s, ec_r)
    early[1] = early[0] + early_in[...]
    dim_start(0, early.at[1], early_dim, er_s, er_r)
    for d in range(1, 8):
        slot = m_in.at[d]
        remote(slot, slot, mr_s.at[d], mr_r.at[d], row_id(me_row)).wait_recv()
    applied = own + msum[me_row]
    for d in range(1, 8):
        applied = applied + m_in[d]
    for h in range(2):
        slot = z_in.at[h]
        remote(slot, slot, rz_s.at[h], rz_r.at[h], {"zh": zo}).wait_recv()
    applied = applied + jnp.concatenate([halves[0] + z_in[0], halves[1] + z_in[1]], axis=0)

    late[0] = pack(wide(exact_dot(applied, applied, NT)))
    core_start(late.at[0], late_in, lc_s, lc_r)
    early[2] = dim_wait(0, early[1], early_dim, er_s, er_r)
    dim_start(1, early.at[2], early_dim, er_s, er_r)
    core_wait(late_in, lc_s, lc_r)
    late[1] = late[0] + late_in[...]
    dim_start(0, late.at[1], late_dim, lr_s, lr_r)
    early[3] = dim_wait(1, early[2], early_dim, er_s, er_r)
    dim_start(2, early.at[3], early_dim, er_s, er_r)
    late[2] = dim_wait(0, late[1], late_dim, lr_s, lr_r)
    dim_start(1, late.at[2], late_dim, lr_s, lr_r)
    sums = dim_wait(2, early[3], early_dim, er_s, er_r)
    late[3] = dim_wait(1, late[2], late_dim, lr_s, lr_r)
    dim_start(2, late.at[3], late_dim, lr_s, lr_r)
    finish(
        state_count, unpack(sums[:8]), unpack(sums[8:]),
        lambda: unpack(dim_wait(2, late[3], late_dim, lr_s, lr_r)),
        vectors, applied, alpha_out, beta_out, next_out,
    )
    for copy in sends:
        copy.wait_send()


def shards(basis, previous, coupling, energies, tile_values, tile_rows, tile_cols, counts):
    state_count = basis.shape[1] * lax.axis_size(ROW) * lax.axis_size(COL)
    f32, i32 = jnp.float32, jnp.int32
    vmem = pl.BlockSpec(memory_space=pltpu.VMEM)
    dma = pltpu.SemaphoreType.DMA
    return pl.pallas_call(
        functools.partial(exchange_kernel, state_count),
        out_shape=(
            jax.ShapeDtypeStruct((K, K), f32),
            jax.ShapeDtypeStruct((K, K), f32),
            jax.ShapeDtypeStruct((K, LEN), f32),
        ),
        in_specs=[pl.BlockSpec(memory_space=pl.ANY)] * 8,
        out_specs=(vmem, vmem, vmem),
        scratch_shapes=[
            pltpu.SMEM((SLOTS,), i32),
            pltpu.SMEM((SLOTS,), i32),
            pltpu.SMEM((1, 1), i32),
            pltpu.SMEM((1, LEN), i32),
            pltpu.VMEM((8, LEN), i32),
            pltpu.VMEM((K, LEN), f32),
            pltpu.VMEM((K, LEN), f32),
            pltpu.VMEM((K, K), f32),
            pltpu.VMEM((1, LEN), f32),
            pltpu.VMEM((SLOTS, LEN, LEN), f32),
            pltpu.VMEM((8, K, LEN), f32),
            pltpu.VMEM((2, 8, 2, 8, HALF, LEN), f32),
            pltpu.VMEM((SLOTS + 1, K, LEN), f32),
            pltpu.VMEM((2, 8, 2, 8, HALF, LEN), f32),
            pltpu.VMEM((2, 2, 2, 4, 8, HALF, LEN), f32),
            pltpu.VMEM((2, 2, 8, HALF, LEN), f32),
            pltpu.VMEM((2, 2, 8, HALF, LEN), f32),
            pltpu.VMEM((2, HALF, LEN), f32),
            pltpu.VMEM((2, HALF, LEN), f32),
            pltpu.VMEM((8, K, LEN), f32),
            pltpu.VMEM((8, K, LEN), f32),
            pltpu.VMEM((4, 16, LEN), f32),
            pltpu.VMEM((16, LEN), f32),
            pltpu.VMEM((3, 8, 16, LEN), f32),
            pltpu.VMEM((4, 8, LEN), f32),
            pltpu.VMEM((8, LEN), f32),
            pltpu.VMEM((3, 8, 8, LEN), f32),
            dma((8,)), dma(()),
            dma((8,)), dma((8,)),
            dma((2,)), dma((2,)),
            dma((2, 2, 8)), dma((2, 2, 8)),
            dma((2, 2, 2, 4)), dma((2, 2, 2, 4)),
            dma((2, 2, 2, 4)), dma((2, 2, 2, 4)),
            dma((2, 2, 8)), dma((2, 2, 8)),
            dma((2,)), dma((2,)),
            dma((8,)), dma((8,)),
            dma(()), dma(()),
            dma((3, 8)), dma((3, 8)),
            dma(()), dma(()),
            dma((3, 8)), dma((3, 8)),
        ],
        compiler_params=pltpu.CompilerParams(
            collective_id=0, has_side_effects=True, vmem_limit_bytes=VMEM_LIMIT
        ),
        name="exchange",
    )(
        tile_rows.reshape(SLOTS), tile_cols.reshape(SLOTS), counts, basis, previous, coupling,
        energies.reshape(1, LEN), tile_values.reshape(SLOTS, LEN, LEN),
    )


def solution(mesh):
    split_mesh = Mesh(mesh.devices.reshape(4, 2, 8, 8, 2), AXES)
    both = ROW + COL
    in_specs = (
        P(None, both),
        P(None, both),
        P(),
        P(both),
        P(ROW, COL, None, None, None),
        P(ROW, COL, None),
        P(ROW, COL, None),
        P(ROW, COL),
    )
    out_specs = (P(), P(), P(None, both))
    return jax.shard_map(
        shards, mesh=split_mesh, in_specs=in_specs, out_specs=out_specs, check_vma=False
    )
```

time: 95.5 us -> 89.5 us (0.937)
  the two profiles are of different devices: /device:TPU:1 before, /device:TPU:2 now
where the time goes in v2:
time: 89.5 us; the launch traced here: 89.1 us
  Pallas kernels  85.1 us (95%)
  local copies, waits for them, and re-layouts  2.66 us (3%)
  between operations  1.3 us (1%)
    pallas_call x1, Pallas kernels, shards(): pl.pallas_call(functools.partial(exchange_kernel, state_count), out_shape...  85.1 us
    unnamed x7, local copies, waits for them, and re-layouts  2.66 us

profile of v2, /device:TPU:2, one launch (start us, length us, event | category | flops | bytes accessed | tf_op | source)
XLA Modules:
  0.0 89.1 jit_solution(11501447019297778255)
XLA Ops:
  1.3 85.1 %exchange.1 = (f32[32,32]{1,0:T(8,128)}, f32[32,32]{1,0:T(8,128)}, f32[32,128]{1,0:T(8,128)}) custom-call(s32[16]{0:T(128)} %bitcast.5, s32[16]{0:T(128)} %bitcast.6, s32[1,1]{1,0:T(1,128)S(6)} %copy.14.count_hbm, f32[32,128]{1,0:T(8,128)} %basis_hbm.1, f32[32,128]{1,0:T(8,128)} %previous_hbm.1, f32[32,32]{1,0:T(8,128)} %coupling_hbm.1, f32[1,128]{1,0:T(1,128)} %bitcast.7, ...), custom_call_target="tpu_custom_call" | custom-call | tf_op jit(solution)/shard_map/exchange/pallas_call | solution.py:420
  86.4 0.0 copy-start.1
  86.4 1.3 %copy.15 = f32[32,32]{1,0:T(8,128)} copy(f32[32,32]{1,0:T(8,128)} %get-tuple-element.6) | data formatting | bytes 8192
  87.8 0.0 copy-done.1
  87.8 0.0 copy-start
  87.8 0.6 copy.16
  88.4 0.1 copy-done
  88.5 0.6 copy.17
Async XLA Ops:
  86.4 1.3 %copy-start.1 = (f32[32,32]{1,0:T(8,128)S(1)}, f32[32,32]{1,0:T(8,128)}, u32[]{:S(2)}) copy-start(f32[32,32]{1,0:T(8,128)} %get-tuple-element.7) | copy-start | bytes 12292
  87.8 0.7 copy-start

commit v3 on v2

--- a/solution.py
+++ b/solution.py
@@ -75,24 +75,61 @@
     residual = applied - exact_dot(alpha_t, vectors, NN)
     alpha_out[...] = alpha
     gram = image_sum() * (1.0 / state_count) - 2.0 * square + projected
+    upper, inverse = factor(gram)
+    beta_out[...] = upper
+    next_out[...] = exact_dot(inverse, residual, NN)
+
+
+def factor(gram):
     at_row = lax.broadcasted_iota(jnp.int32, (K, K), 0)
     at_col = lax.broadcasted_iota(jnp.int32, (K, K), 1)
-    eye = jnp.where(at_row == at_col, 1.0, 0.0)
-    work = jnp.concatenate([gram, eye], axis=1)
-    index = lax.broadcasted_iota(jnp.int32, (K, 2 * K), 0)
-    for j in range(K):
-        scale = 1.0 / jnp.sqrt(work[j : j + 1, j : j + 1])
-        row = work[j : j + 1, :] * scale
-        column = work[:, j : j + 1] * scale
-        work = jnp.where(index > j, work - column * row, jnp.where(index == j, row, work))
-    beta_out[...] = jnp.where(at_row <= at_col, work[:, :K], 0.0)
-    next_out[...] = exact_dot(work[:, K:], residual, NN)
+    work = jnp.concatenate([gram, jnp.where(at_row == at_col, 1.0, 0.0)], axis=1)
+    done = []
+    sub = lax.broadcasted_iota(jnp.int32, (8, 2 * K), 0)
+    for q in range(4):
+        block = work[:8]
+        rest = work[8:]
+        left = 24 - 8 * q
+        heads = [jnp.broadcast_to(block[:, 8 * q + k : 8 * q + k + 1], (8, 2 * K)) for k in range(8)]
+        rows = [jnp.broadcast_to(block[k : k + 1, :], (8, 2 * K)) for k in range(8)]
+        full = {}
+        for k in range(8):
+            for m in range(k, 8):
+                full[k, m] = jnp.broadcast_to(heads[m][k : k + 1, :], (8, 2 * K))
+        if left:
+            cols = [
+                jnp.broadcast_to(rest[:, 8 * q + k : 8 * q + k + 1], (left, 2 * K)).reshape(left // 8, 8, 2 * K)
+                for k in range(8)
+            ]
+            rest = rest.reshape(left // 8, 8, 2 * K)
+        out = jnp.zeros((8, 2 * K), jnp.float32)
+        for k in range(8):
+            pivot = full[k, k]
+            scale = 1.0 / pivot
+            root = lax.rsqrt(pivot)
+            root = root * (1.5 - 0.5 * pivot * root * root)
+            out = jnp.where(sub == k, rows[k] * root, out)
+            factors = {m: full[k, m] * scale for m in range(k + 1, 8)}
+            for m in range(k + 1, 8):
+                for n in range(m, 8):
+                    full[m, n] = full[m, n] - full[k, n] * factors[m]
+            for m in range(k + 1, 8):
+                rows[m] = rows[m] - rows[k] * factors[m]
+            if left:
+                rest = rest - cols[k] * (rows[k] * scale)[None]
+                for m in range(k + 1, 8):
+                    cols[m] = cols[m] - cols[k] * factors[m][None]
+        done.append(out)
+        if left:
+            work = rest.reshape(left, 2 * K)
+    both = jnp.concatenate(done, axis=0)
+    return jnp.where(at_row <= at_col, both[:, :K], 0.0), both[:, K:]
 
 
 def exchange_kernel(
     state_count,
     rows_hbm, cols_hbm, count_hbm, basis_hbm, previous_hbm, coupling_hbm, energies_hbm, tiles_hbm,
-    alpha_out, beta_out, next_out,
+    out,
     rows, cols, count, inv, inv_lanes, basis, previous, coupling, energies,
     tiles, cstates, rstates, direct, part, ring_in, last, last_in, mid, z_in, msum, m_in,
     early, early_in, early_dim, late, late_in, late_dim,
@@ -111,22 +148,10 @@
     order = (4, 3, 5, 2, 6, 1, 7)
 
     def row_id(r):
-        return {"zl": r // 2, "co": r % 2}
+        return {"zl": lax.div(r, 2), "co": lax.rem(r, 2)}
 
     def z_id(z):
-        return {"zh": z // 4, "zl": z % 4}
-
-    barrier = pltpu.get_barrier_semaphore()
-
-    def hello(where):
-        pl.semaphore_signal(barrier, inc=1, device_id=where, device_id_type=MESH)
-
-    for d in order:
-        hello({"x": (x + d) % 8})
-        hello({"y": (y + d) % 8})
-        hello(row_id((me_row + d) % 8))
-    for d in range(4):
-        hello({"zh": zo, "zl": (zl + d) % 4})
+        return {"zh": lax.div(z, 4), "zl": lax.rem(z, 4)}
 
     loads = [
         pltpu.make_async_copy(src, dst, in_sem.at[i])
@@ -137,13 +162,48 @@
             )
         )
     ]
-    for copy in loads:
+    loads[0].start()
+    barrier = pltpu.get_barrier_semaphore()
+
+    def hello(where):
+        pl.semaphore_signal(barrier, inc=1, device_id=where, device_id_type=MESH)
+
+    for d in order:
+        hello({"x": lax.rem(x + d, 8)})
+        hello({"y": lax.rem(y + d, 8)})
+        hello(row_id(lax.rem(me_row + d, 8)))
+    for d in range(4):
+        hello({"zh": zo, "zl": lax.rem(zl + d, 4)})
+
+    for copy in loads[1:]:
         copy.start()
     direct[SLOTS] = jnp.zeros((K, LEN), jnp.float32)
     loads[0].wait()
     for h in range(2):
         rstates[h, ring_pos[h], zh, exch_pos[h]] = basis[h * HALF : (h + 1) * HALF, :]
     cstates[me_row] = basis[...]
+    pl.semaphore_wait(barrier, 25)
+
+    sends = []
+
+    def go(copy):
+        copy.start()
+        sends.append(copy)
+
+    for h in range(2):
+        slot = rstates.at[h, ring_pos[h], zh, exch_pos[h]]
+        go(remote(basis.at[pl.ds(h * HALF, HALF)], slot, z0_s.at[h], z0_r.at[h], {"zh": zo}))
+    for d in order:
+        for h in range(2):
+            slot = rstates.at[h, ring_pos[h], zh, exch_pos[h]]
+            go(
+                remote(
+                    basis.at[pl.ds(h * HALF, HALF)], slot, ex_s.at[h, 0, d], ex_r.at[h, 0, d],
+                    {exch_axis[h]: lax.rem(exch_pos[h] + d, 8)},
+                )
+            )
+        go(remote(basis, cstates.at[me_row], rg_s.at[d], rg_r.at[d], row_id(lax.rem(me_row + d, 8))))
+
     loads[1].wait()
     loads[2].wait()
     live = count[0, 0]
@@ -154,32 +214,11 @@
     inv_lanes[...] = table
     inv_copy = pltpu.make_async_copy(inv_lanes.at[pl.ds(0, 1)], inv, inv_sem)
     inv_copy.start()
-    pl.semaphore_wait(barrier, 25)
-
-    sends = []
-
-    def go(copy):
-        copy.start()
-        sends.append(copy)
-
-    for h in range(2):
-        slot = rstates.at[h, ring_pos[h], zh, exch_pos[h]]
-        go(remote(basis.at[pl.ds(h * HALF, HALF)], slot, z0_s.at[h], z0_r.at[h], {"zh": zo}))
-    for d in order:
-        for h in range(2):
-            slot = rstates.at[h, ring_pos[h], zh, exch_pos[h]]
-            go(
-                remote(
-                    basis.at[pl.ds(h * HALF, HALF)], slot, ex_s.at[h, 0, d], ex_r.at[h, 0, d],
-                    {exch_axis[h]: (exch_pos[h] + d) % 8},
-                )
-            )
-        go(remote(basis, cstates.at[me_row], rg_s.at[d], rg_r.at[d], row_id((me_row + d) % 8)))
 
     def exch_wait(h, c):
         zc = (zh, zo)[c]
         for d in range(1, 8):
-            slot = rstates.at[h, ring_pos[h], zc, (exch_pos[h] + 8 - d) % 8]
+            slot = rstates.at[h, ring_pos[h], zc, lax.rem(exch_pos[h] + 8 - d, 8)]
             remote(slot, slot, ex_s.at[h, c, d], ex_r.at[h, c, d], {exch_axis[h]: exch_pos[h]}).wait_recv()
 
     def hops(sign, c):
@@ -188,19 +227,19 @@
     def ag_copy(h, g, c, s):
         sign = (1, -1)[g]
         zc = (zh, zo)[c]
-        slot = rstates.at[h, (ring_pos[h] + 8 - sign * (s - 1)) % 8, zc]
+        slot = rstates.at[h, lax.rem(ring_pos[h] + 8 - sign * (s - 1), 8), zc]
         return remote(
             slot, slot, ag_s.at[h, g, c, s - 1], ag_r.at[h, g, c, s - 1],
-            {ring_axis[h]: (ring_pos[h] + 8 + sign) % 8},
+            {ring_axis[h]: lax.rem(ring_pos[h] + 8 + sign, 8)},
         )
 
     def ag_wait(h, g, c, s):
         sign = (1, -1)[g]
         zc = (zh, zo)[c]
-        slot = rstates.at[h, (ring_pos[h] + 8 - sign * s) % 8, zc]
+        slot = rstates.at[h, lax.rem(ring_pos[h] + 8 - sign * s, 8), zc]
         remote(
             slot, slot, ag_s.at[h, g, c, s - 1], ag_r.at[h, g, c, s - 1],
-            {ring_axis[h]: (ring_pos[h] + 8 + sign) % 8},
+            {ring_axis[h]: lax.rem(ring_pos[h] + 8 + sign, 8)},
         ).wait_recv()
 
     for h in range(2):
@@ -210,7 +249,7 @@
             go(
                 remote(
                     slot, slot, ex_s.at[h, 1, d], ex_r.at[h, 1, d],
-                    {exch_axis[h]: (exch_pos[h] + d) % 8},
+                    {exch_axis[h]: lax.rem(exch_pos[h] + d, 8)},
                 )
             )
     for h in range(2):
@@ -219,7 +258,7 @@
             go(ag_copy(h, g, 0, 1))
 
     for d in range(1, 8):
-        slot = cstates.at[(me_row + 8 - d) % 8]
+        slot = cstates.at[lax.rem(me_row + 8 - d, 8)]
         remote(slot, slot, rg_s.at[d], rg_r.at[d], row_id(me_row)).wait_recv()
     for copy in loads[3:]:
         copy.wait()
@@ -241,10 +280,10 @@
     def rs_copy(h, g, c, s):
         sign = (1, -1)[g]
         zc = (zo, zh)[c]
-        slot = part.at[h, (ring_pos[h] + 8 + sign * (5 - s)) % 8, zc]
+        slot = part.at[h, lax.rem(ring_pos[h] + 8 + sign * (5 - s), 8), zc]
         return remote(
             slot, ring_in.at[h, g, c, s - 1], rs_s.at[h, g, c, s - 1], rs_r.at[h, g, c, s - 1],
-            {ring_axis[h]: (ring_pos[h] + 8 + sign) % 8},
+            {ring_axis[h]: lax.rem(ring_pos[h] + 8 + sign, 8)},
         )
 
     def rs_wait(h, g, c, s):
@@ -252,7 +291,7 @@
         sign = (1, -1)[g]
         remote(
             slot, slot, rs_s.at[h, g, c, s - 1], rs_r.at[h, g, c, s - 1],
-            {ring_axis[h]: (ring_pos[h] + 8 + sign) % 8},
+            {ring_axis[h]: lax.rem(ring_pos[h] + 8 + sign, 8)},
         ).wait_recv()
 
     def rs_step(c, s):
@@ -268,7 +307,7 @@
                 if n == 4 or s > 1:
                     rs_wait(h, g, c, s)
                 if s < 4:
-                    to = (ring_pos[h] + 8 + sign * (4 - s)) % 8
+                    to = lax.rem(ring_pos[h] + 8 + sign * (4 - s), 8)
                     if n == 4 or s > 1:
                         part[h, to, zc] = part[h, to, zc] + ring_in[h, g, c, s - 1]
                     go(rs_copy(h, g, c, s + 1))
@@ -278,7 +317,7 @@
         for h in range(2):
             last[h, c] = part[h, ring_pos[h], zc] + (ring_in[h, 0, c, 3] + ring_in[h, 1, c, 3])
             for d in order:
-                to = (exch_pos[h] + d) % 8
+                to = lax.rem(exch_pos[h] + d, 8)
                 go(
                     remote(
                         last.at[h, c, to], last_in.at[h, c, d], rx_s.at[h, c, d], rx_r.at[h, c, d],
@@ -286,44 +325,91 @@
                     )
                 )
 
-    def ag_step(s):
-        for c in range(2):
-            for h in range(2):
-                for g in range(2):
-                    n = hops((1, -1)[g], c)
-                    if s <= n:
-                        ag_wait(h, g, c, s)
-                        if s < n:
-                            go(ag_copy(h, g, c, s + 1))
+    def ag_flow(c, s):
+        for h in range(2):
+            for g in range(2):
+                n = hops((1, -1)[g], c)
+                if s <= n:
+                    ag_wait(h, g, c, s)
+                    if s < n:
+                        go(ag_copy(h, g, c, s + 1))
+
+    mirror = []
+    row_parts = []
+
+    def mirror_step(tiles_from, tiles_to):
+        for s in range(tiles_from, tiles_to):
+            t = rows[s]
+            at_y, at_x, at_z = lax.div(t, 16), lax.rem(lax.div(t, 2), 8), lax.rem(t, 2)
+            picked = split(
+                jnp.concatenate([rstates[0, at_y, at_z, at_x], rstates[1, at_x, at_z, at_y]], axis=0)
+            )
+            row_parts.append(picked)
+            mirror.append(dot_three(picked, split(tiles[s]), NN))
+
+    def drain():
+        while sends:
+            sends.pop(0).wait_send()
 
     rs_step(0, 0)
-    for s in range(1, 5):
-        ag_step(s)
+    ag_flow(0, 1)
+    rs_step(1, 0)
+    rs_step(0, 1)
+    ag_flow(1, 1)
+    for s in range(2, 5):
+        ag_flow(0, s)
+        rs_step(0, s)
+        if s == 4:
+            rs_last(0)
         rs_step(1, s - 1)
-        rs_step(0, s)
-    rs_last(0)
+        ag_flow(1, s)
+    mirror_step(0, 8)
     rs_step(1, 4)
     rs_last(1)
-
-    mirror = []
-    row_parts = []
-    for s in range(SLOTS):
-        t = rows[s]
-        at_y, at_x, at_z = t // 16, (t // 2) % 8, t % 2
-        picked = split(
-            jnp.concatenate([rstates[0, at_y, at_z, at_x], rstates[1, at_x, at_z, at_y]], axis=0)
-        )
-        row_parts.append(picked)
-        mirror.append(dot_three(picked, split(tiles[s]), NN))
+    mirror_step(8, SLOTS)
+    weights = [[jnp.where((cols[s] == u) & (s < live), 1.0, 0.0) for s in range(SLOTS)] for u in range(8)]
     for u in range(8):
-        total = jnp.zeros((K, LEN), jnp.float32)
-        for s in range(SLOTS):
-            weight = jnp.where((cols[s] == u) & (s < live), 1.0, 0.0)
-            total = total + weight * mirror[s]
+        total = weights[u][0] * mirror[0]
+        for s in range(1, SLOTS):
+            total = total + weights[u][s] * mirror[s]
         msum[u] = total
     for d in order:
-        to = (me_row + d) % 8
+        to = lax.rem(me_row + d, 8)
         go(remote(msum.at[to], m_in.at[d], mr_s.at[d], mr_r.at[d], row_id(to)))
+
+    def last_sum(c, h):
+        total = last[h, c, exch_pos[h]]
+        for d in range(1, 8):
+            slot = last_in.at[h, c, d]
+            remote(slot, slot, rx_s.at[h, c, d], rx_r.at[h, c, d], {exch_axis[h]: exch_pos[h]}).wait_recv()
+            total = total + last_in[h, c, d]
+        return total
+
+    for h in range(2):
+        mid[h] = last_sum(0, h)
+        go(remote(mid.at[h], z_in.at[h], rz_s.at[h], rz_r.at[h], {"zh": zo}))
+
+    def core_start(src, dst, send, recv):
+        go(remote(src, dst, send, recv, {"co": 1 - co}))
+
+    def core_wait(dst, send, recv):
+        remote(dst, dst, send, recv, {"co": 1 - co}).wait_recv()
+
+    def dim_start(dim, src, dst, send, recv):
+        for d in order:
+            where = ({"x": lax.rem(x + d, 8)}, {"y": lax.rem(y + d, 8)}, z_id(lax.rem(me_z + d, 8)))[dim]
+            go(remote(src, dst.at[dim, d], send.at[dim, d], recv.at[dim, d], where))
+
+    def dim_wait(dim, mine, dst, send, recv):
+        for d in range(1, 8):
+            slot = dst.at[dim, d]
+            remote(slot, slot, send.at[dim, d], recv.at[dim, d], {"x": x}).wait_recv()
+        dst[dim, 0] = mine
+        here = (x, y, me_z)[dim]
+        total = dst[dim, here]
+        for k in range(1, 8):
+            total = total + dst[dim, lax.rem(here + 8 - k, 8)]
+        return total
 
     vectors = basis[...]
     own = energies[...] * vectors - exact_dot(coupling[...], previous[...], NN)
@@ -337,44 +423,8 @@
     cross = cross + cross.T + exact_dot(vectors, own, NT)
     early[0, :8] = pack(wide(cross))
     early[0, 8:] = pack(wide(exact_dot(vectors, vectors, NT)))
-
-    def core_start(src, dst, send, recv):
-        go(remote(src, dst, send, recv, {"co": 1 - co}))
-
-    def core_wait(dst, send, recv):
-        remote(dst, dst, send, recv, {"co": 1 - co}).wait_recv()
-
-    def dim_start(dim, src, dst, send, recv):
-        for d in order:
-            where = ({"x": (x + d) % 8}, {"y": (y + d) % 8}, z_id((me_z + d) % 8))[dim]
-            go(remote(src, dst.at[dim, d], send.at[dim, d], recv.at[dim, d], where))
-
-    def dim_wait(dim, mine, dst, send, recv):
-        for d in range(1, 8):
-            slot = dst.at[dim, d]
-            remote(slot, slot, send.at[dim, d], recv.at[dim, d], {"x": x}).wait_recv()
-        dst[dim, 0] = mine
-        here = (x, y, me_z)[dim]
-        total = dst[dim, here]
-        for k in range(1, 8):
-            total = total + dst[dim, (here + 8 - k) % 8]
-        return total
-
     core_start(early.at[0], early_in, ec_s, ec_r)
-
-    halves = []
-    for c in range(2):
-        for h in range(2):
-            total = last[h, c, exch_pos[h]]
-            for d in range(1, 8):
-                slot = last_in.at[h, c, d]
-                remote(slot, slot, rx_s.at[h, c, d], rx_r.at[h, c, d], {exch_axis[h]: exch_pos[h]}).wait_recv()
-                total = total + last_in[h, c, d]
-            if c == 0:
-                mid[h] = total
-                go(remote(mid.at[h], z_in.at[h], rz_s.at[h], rz_r.at[h], {"zh": zo}))
-            else:
-                halves.append(total)
+    halves = [last_sum(1, h) for h in range(2)]
     core_wait(early_in, ec_s, ec_r)
     early[1] = early[0] + early_in[...]
     dim_start(0, early.at[1], early_dim, er_s, er_r)
@@ -391,25 +441,31 @@
 
     late[0] = pack(wide(exact_dot(applied, applied, NT)))
     core_start(late.at[0], late_in, lc_s, lc_r)
-    early[2] = dim_wait(0, early[1], early_dim, er_s, er_r)
-    dim_start(1, early.at[2], early_dim, er_s, er_r)
     core_wait(late_in, lc_s, lc_r)
     late[1] = late[0] + late_in[...]
     dim_start(0, late.at[1], late_dim, lr_s, lr_r)
+    early[2] = dim_wait(0, early[1], early_dim, er_s, er_r)
+    dim_start(1, early.at[2], early_dim, er_s, er_r)
+    late[2] = dim_wait(0, late[1], late_dim, lr_s, lr_r)
+    dim_start(1, late.at[2], late_dim, lr_s, lr_r)
     early[3] = dim_wait(1, early[2], early_dim, er_s, er_r)
     dim_start(2, early.at[3], early_dim, er_s, er_r)
-    late[2] = dim_wait(0, late[1], late_dim, lr_s, lr_r)
-    dim_start(1, late.at[2], late_dim, lr_s, lr_r)
-    sums = dim_wait(2, early[3], early_dim, er_s, er_r)
+    drain()
     late[3] = dim_wait(1, late[2], late_dim, lr_s, lr_r)
     dim_start(2, late.at[3], late_dim, lr_s, lr_r)
+    sums = dim_wait(2, early[3], early_dim, er_s, er_r)
     finish(
         state_count, unpack(sums[:8]), unpack(sums[8:]),
         lambda: unpack(dim_wait(2, late[3], late_dim, lr_s, lr_r)),
-        vectors, applied, alpha_out, beta_out, next_out,
-    )
-    for copy in sends:
-        copy.wait_send()
+        vectors, applied, out.at[pl.ds(K, K), pl.ds(0, K)], out.at[pl.ds(2 * K, K), pl.ds(0, K)], out.at[pl.ds(0, K)],
+    )
+    drain()
+
+
+def deliver_kernel(packed, alpha_out, beta_out, next_out):
+    next_out[...] = packed[:K, :]
+    alpha_out[...] = packed[K : 2 * K, :K]
+    beta_out[...] = packed[2 * K :, :K]
 
 
 def shards(basis, previous, coupling, energies, tile_values, tile_rows, tile_cols, counts):
@@ -417,15 +473,11 @@
     f32, i32 = jnp.float32, jnp.int32
     vmem = pl.BlockSpec(memory_space=pltpu.VMEM)
     dma = pltpu.SemaphoreType.DMA
-    return pl.pallas_call(
+    out = pl.pallas_call(
         functools.partial(exchange_kernel, state_count),
-        out_shape=(
-            jax.ShapeDtypeStruct((K, K), f32),
-            jax.ShapeDtypeStruct((K, K), f32),
-            jax.ShapeDtypeStruct((K, LEN), f32),
-        ),
+        out_shape=jax.ShapeDtypeStruct((3 * K, LEN), f32),
         in_specs=[pl.BlockSpec(memory_space=pl.ANY)] * 8,
-        out_specs=(vmem, vmem, vmem),
+        out_specs=vmem,
         scratch_shapes=[
             pltpu.SMEM((SLOTS,), i32),
             pltpu.SMEM((SLOTS,), i32),
@@ -476,6 +528,18 @@
         tile_rows.reshape(SLOTS), tile_cols.reshape(SLOTS), counts, basis, previous, coupling,
         energies.reshape(1, LEN), tile_values.reshape(SLOTS, LEN, LEN),
     )
+    return pl.pallas_call(
+        deliver_kernel,
+        out_shape=(
+            jax.ShapeDtypeStruct((K, K), f32),
+            jax.ShapeDtypeStruct((K, K), f32),
+            jax.ShapeDtypeStruct((K, LEN), f32),
+        ),
+        in_specs=[vmem],
+        out_specs=(vmem, vmem, vmem),
+        compiler_params=pltpu.CompilerParams(vmem_limit_bytes=VMEM_LIMIT),
+        name="deliver",
+    )(out)
 
 
 def solution(mesh):

time: 89.5 us -> 83.2 us (0.930)
  the two profiles are of different devices: /device:TPU:2 before, /device:TPU:1 now
where the time goes in v3:
time: 83.2 us; the launch traced here: 82.9 us
  Pallas kernels  81.7 us (98%)
  between operations  1.29 us (2%)
    pallas_call x1, Pallas kernels, shards(): pl.pallas_call(functools.partial(exchange_kernel, state_count), out_shape...  80.2 us

profile of v3, /device:TPU:1, one launch (start us, length us, event | category | flops | bytes accessed | tf_op | source)
XLA Modules:
  0.0 82.9 jit_solution(6168628794713946281)
XLA Ops:
  1.3 80.2 %exchange.1.packed = f32[96,128]{1,0:T(8,128)} custom-call(s32[16]{0:T(128)} %bitcast.5, s32[16]{0:T(128)} %bitcast.6, s32[1,1]{1,0:T(1,128)S(6)} %copy.11.count_hbm, f32[32,128]{1,0:T(8,128)} %basis_hbm.1, f32[32,128]{1,0:T(8,128)} %previous_hbm.1, f32[32,32]{1,0:T(8,128)} %coupling_hbm.1, f32[1,128]{1,0:T(1,128)} %bitcast.7, f32[16,128,128]{2,1,0:T(8,128)} %bitcast.4), custom_call_target="tpu_custom_call" | custom-call | tf_op jit(solution)/shard_map/exchange/pallas_call | solution.py:476
  81.5 1.4 %deliver.1 = (f32[32,32]{1,0:T(8,128)}, f32[32,32]{1,0:T(8,128)}, f32[32,128]{1,0:T(8,128)}) custom-call(f32[96,128]{1,0:T(8,128)} %exchange.1.packed), custom_call_target="tpu_custom_call" | custom-call | tf_op jit(solution)/shard_map/deliver/pallas_call | solution.py:531

commit v4 on v3

--- a/solution.py
+++ b/solution.py
@@ -265,10 +265,6 @@
     inv_copy.wait()
     for s in range(SLOTS):
         direct[s] = dot_three(split(cstates[cols[s]]), split(tiles[s]), NT)
-    for h in range(2):
-        exch_wait(h, 1)
-        for g in range(2):
-            go(ag_copy(h, g, 1, 1))
 
     for a in range(8):
         for b in range(8):
@@ -354,6 +350,10 @@
     rs_step(0, 0)
     ag_flow(0, 1)
     rs_step(1, 0)
+    for h in range(2):
+        exch_wait(h, 1)
+        for g in range(2):
+            go(ag_copy(h, g, 1, 1))
     rs_step(0, 1)
     ag_flow(1, 1)
     for s in range(2, 5):
@@ -363,10 +363,7 @@
             rs_last(0)
         rs_step(1, s - 1)
         ag_flow(1, s)
-    mirror_step(0, 8)
-    rs_step(1, 4)
-    rs_last(1)
-    mirror_step(8, SLOTS)
+    mirror_step(0, SLOTS)
     weights = [[jnp.where((cols[s] == u) & (s < live), 1.0, 0.0) for s in range(SLOTS)] for u in range(8)]
     for u in range(8):
         total = weights[u][0] * mirror[0]
@@ -376,18 +373,6 @@
     for d in order:
         to = lax.rem(me_row + d, 8)
         go(remote(msum.at[to], m_in.at[d], mr_s.at[d], mr_r.at[d], row_id(to)))
-
-    def last_sum(c, h):
-        total = last[h, c, exch_pos[h]]
-        for d in range(1, 8):
-            slot = last_in.at[h, c, d]
-            remote(slot, slot, rx_s.at[h, c, d], rx_r.at[h, c, d], {exch_axis[h]: exch_pos[h]}).wait_recv()
-            total = total + last_in[h, c, d]
-        return total
-
-    for h in range(2):
-        mid[h] = last_sum(0, h)
-        go(remote(mid.at[h], z_in.at[h], rz_s.at[h], rz_r.at[h], {"zh": zo}))
 
     def core_start(src, dst, send, recv):
         go(remote(src, dst, send, recv, {"co": 1 - co}))
@@ -424,10 +409,25 @@
     early[0, :8] = pack(wide(cross))
     early[0, 8:] = pack(wide(exact_dot(vectors, vectors, NT)))
     core_start(early.at[0], early_in, ec_s, ec_r)
-    halves = [last_sum(1, h) for h in range(2)]
+    rs_step(1, 4)
+    rs_last(1)
+
+    def last_sum(c, h):
+        total = last[h, c, exch_pos[h]]
+        for d in range(1, 8):
+            slot = last_in.at[h, c, d]
+            remote(slot, slot, rx_s.at[h, c, d], rx_r.at[h, c, d], {exch_axis[h]: exch_pos[h]}).wait_recv()
+            total = total + last_in[h, c, d]
+        return total
+
+    for h in range(2):
+        mid[h] = last_sum(0, h)
+        go(remote(mid.at[h], z_in.at[h], rz_s.at[h], rz_r.at[h], {"zh": zo}))
+
     core_wait(early_in, ec_s, ec_r)
     early[1] = early[0] + early_in[...]
     dim_start(0, early.at[1], early_dim, er_s, er_r)
+    halves = [last_sum(1, h) for h in range(2)]
     for d in range(1, 8):
         slot = m_in.at[d]
         remote(slot, slot, mr_s.at[d], mr_r.at[d], row_id(me_row)).wait_recv()

time: 83.2 us -> 80.9 us (0.972)
  Pallas kernels: 81.7 us -> 79.4 us
    pallas_call x1, Pallas kernels: 80.2 us -> 77.9 us  [shards(): pl.pallas_call(functools.partial(exchange_kernel, state_count), out_shape...]
where the time goes in v4:
time: 80.9 us; the launch traced here: 80.7 us
  Pallas kernels  79.4 us (98%)
  between operations  1.29 us (2%)
    pallas_call x1, Pallas kernels, shards(): pl.pallas_call(functools.partial(exchange_kernel, state_count), out_shape...  77.9 us

profile of v4, /device:TPU:1, one launch (start us, length us, event | category | flops | bytes accessed | tf_op | source)
XLA Modules:
  0.0 80.7 jit_solution(7128756936845005950)
XLA Ops:
  1.3 77.9 %exchange.1.packed = f32[96,128]{1,0:T(8,128)} custom-call(s32[16]{0:T(128)} %bitcast.5, s32[16]{0:T(128)} %bitcast.6, s32[1,1]{1,0:T(1,128)S(6)} %copy.11.count_hbm, f32[32,128]{1,0:T(8,128)} %basis_hbm.1, f32[32,128]{1,0:T(8,128)} %previous_hbm.1, f32[32,32]{1,0:T(8,128)} %coupling_hbm.1, f32[1,128]{1,0:T(1,128)} %bitcast.7, f32[16,128,128]{2,1,0:T(8,128)} %bitcast.4), custom_call_target="tpu_custom_call" | custom-call | tf_op jit(solution)/shard_map/exchange/pallas_call | solution.py:476
  79.2 1.4 %deliver.1 = (f32[32,32]{1,0:T(8,128)}, f32[32,32]{1,0:T(8,128)}, f32[32,128]{1,0:T(8,128)}) custom-call(f32[96,128]{1,0:T(8,128)} %exchange.1.packed), custom_call_target="tpu_custom_call" | custom-call | tf_op jit(solution)/shard_map/deliver/pallas_call | solution.py:531

commit v5 on v4

--- a/solution.py
+++ b/solution.py
@@ -214,6 +214,12 @@
     inv_lanes[...] = table
     inv_copy = pltpu.make_async_copy(inv_lanes.at[pl.ds(0, 1)], inv, inv_sem)
     inv_copy.start()
+    vectors = basis[...]
+    for copy in loads[3:]:
+        copy.wait()
+    own = energies[...] * vectors - exact_dot(coupling[...], previous[...], NN)
+    early[0, 8:] = pack(wide(exact_dot(vectors, vectors, NT)))
+    own_cross = exact_dot(vectors, own, NT)
 
     def exch_wait(h, c):
         zc = (zh, zo)[c]
@@ -260,8 +266,6 @@
     for d in range(1, 8):
         slot = cstates.at[lax.rem(me_row + 8 - d, 8)]
         remote(slot, slot, rg_s.at[d], rg_r.at[d], row_id(me_row)).wait_recv()
-    for copy in loads[3:]:
-        copy.wait()
     inv_copy.wait()
     for s in range(SLOTS):
         direct[s] = dot_three(split(cstates[cols[s]]), split(tiles[s]), NT)
@@ -396,8 +400,6 @@
             total = total + dst[dim, lax.rem(here + 8 - k, 8)]
         return total
 
-    vectors = basis[...]
-    own = energies[...] * vectors - exact_dot(coupling[...], previous[...], NN)
     live_direct = [split(jnp.where(s < live, 1.0, 0.0) * direct[s]) for s in range(SLOTS)]
     rh = jnp.concatenate([p[0] for p in row_parts], axis=1)
     rl = jnp.concatenate([p[1] for p in row_parts], axis=1)
@@ -405,9 +407,8 @@
     dl = jnp.concatenate([p[1] for p in live_direct], axis=1)
     cross = lax.dot_general(jnp.concatenate([rh, rl], axis=0), dh, NT, preferred_element_type=jnp.float32)
     cross = cross[:K] + (cross[K:] + lax.dot_general(rh, dl, NT, preferred_element_type=jnp.float32))
-    cross = cross + cross.T + exact_dot(vectors, own, NT)
+    cross = cross + cross.T + own_cross
     early[0, :8] = pack(wide(cross))
-    early[0, 8:] = pack(wide(exact_dot(vectors, vectors, NT)))
     core_start(early.at[0], early_in, ec_s, ec_r)
     rs_step(1, 4)
     rs_last(1)

time: 80.9 us -> 80.9 us (level)
  no operation moved by 1% of the time
where the time goes in v5:
time: 80.9 us; the launch traced here: 80.7 us
  Pallas kernels  79.4 us (98%)
  between operations  1.29 us (2%)
    pallas_call x1, Pallas kernels, shards(): pl.pallas_call(functools.partial(exchange_kernel, state_count), out_shape...  78 us

profile of v5, /device:TPU:1, one launch (start us, length us, event | category | flops | bytes accessed | tf_op | source)
XLA Modules:
  0.0 80.7 jit_solution(13076449102213500387)
XLA Ops:
  1.3 78.0 %exchange.1.packed = f32[96,128]{1,0:T(8,128)} custom-call(s32[16]{0:T(128)} %bitcast.5, s32[16]{0:T(128)} %bitcast.6, s32[1,1]{1,0:T(1,128)S(6)} %copy.11.count_hbm, f32[32,128]{1,0:T(8,128)} %basis_hbm.1, f32[32,128]{1,0:T(8,128)} %previous_hbm.1, f32[32,32]{1,0:T(8,128)} %coupling_hbm.1, f32[1,128]{1,0:T(1,128)} %bitcast.7, f32[16,128,128]{2,1,0:T(8,128)} %bitcast.4), custom_call_target="tpu_custom_call" | custom-call | tf_op jit(solution)/shard_map/exchange/pallas_call | solution.py:477
  79.2 1.4 %deliver.1 = (f32[32,32]{1,0:T(8,128)}, f32[32,32]{1,0:T(8,128)}, f32[32,128]{1,0:T(8,128)}) custom-call(f32[96,128]{1,0:T(8,128)} %exchange.1.packed), custom_call_target="tpu_custom_call" | custom-call | tf_op jit(solution)/shard_map/deliver/pallas_call | solution.py:532
